TPU v7x, 256 devices: a whole 4x4x8 slice. The times are simulated.
256 devices in a mesh: pairs: 32 (over z, y), aux: 8 (over x, core).
Axes of the slice: x: 4, y: 4, z: 8, core: 2. Of those that a mesh axis runs over, the one named last changes fastest.
Arguments:
- cholesky_slab: bfloat16 [8192, 35840], P('pairs', 'aux'), may hold values from -40 to 40, as said below
- test_matrix: bfloat16 [35840, 768], P('aux', 'pairs'), may hold values from -0.03125 to 0.03125
Outputs:
- projected: float32 [768, 35840], P('pairs', 'aux')
Inputs may be any that keep to these rules, and one draw needn't show every extreme that they name: cholesky_slab: real entries with varying row and column magnitudes.
All inputs are finite; a program needn't handle non-finite values.
Results may differ from a plain program's by a relative error of at most 0.0003.
Values may be sent and summed in bfloat16 or wider, within the bound.
A program may use at most 64 MiB of HBM per device.

v0:
```python
import jax
import jax.numpy as jnp
from jax import lax
from jax.sharding import Mesh
from jax.sharding import PartitionSpec as P

PAIRS = ("pairs_0", "pairs_1")


def whole_of(x, axes, dim):
    for axis in reversed(axes):
        x = lax.all_gather(x, axis, axis=dim, tiled=True)
    return x


def total_of_pieces(x, axis):
    return lax.all_gather(x, axis).sum(0)


def padded_to(lines, count):
    spare = -lines.shape[0] % count
    if not spare:
        return lines
    return jnp.concatenate([lines, jnp.zeros((spare, *lines.shape[1:]), lines.dtype)])


def own_block(blocks, axes, turns):
    inside = blocks.shape[1:]
    blocks = blocks.reshape(*(lax.axis_size(a) for a in axes), *inside)
    blocks = jnp.moveaxis(blocks, turns, range(len(axes))).reshape(-1, *inside)
    for k in turns:
        blocks = lax.psum_scatter(blocks, axes[k], scatter_dimension=0, tiled=True)
    return blocks[0]


def gather_in_order(x, axes, turns):
    blocks = x[None]
    for k in turns:
        blocks = lax.all_gather(blocks, axes[k], axis=0, tiled=True)
    block = [lax.axis_size(axes[k]) for k in reversed(turns)]
    blocks = blocks.reshape(*block, *x.shape)
    turned = sorted(range(len(turns)), key=lambda place: turns[len(turns) - 1 - place])
    return blocks.transpose(*turned, *range(len(turns), blocks.ndim)).reshape(-1, *x.shape)


def total_of(x, axes, turns):
    count, lines = (lax.axis_size(axes), x.reshape(-1, *x.shape[1:][-1:]))
    blocks = padded_to(lines, count).reshape(count, -1, *lines.shape[1:])
    own = own_block(blocks, axes, turns)
    whole = gather_in_order(own, axes, turns[::-1]).reshape(-1, *lines.shape[1:])
    return whole[: len(lines)].reshape(x.shape)


def sum_by_axis(total, axes):
    for axis in axes:
        total = lax.psum_scatter(total, axis, scatter_dimension=0, tiled=True)
    return total


def gram_local(sketch_part):
    return jnp.dot(
        sketch_part.T,
        sketch_part,
        precision=lax.Precision.HIGHEST,
        preferred_element_type=jnp.float32,
    )


def basis_from(gram_matrix, sketch_part):
    lower_factor = jnp.linalg.cholesky(gram_matrix)
    return jax.scipy.linalg.solve_triangular(lower_factor, sketch_part.T, lower=True)


def body(cholesky_slab, test_matrix):
    partial_value = jnp.dot(
        cholesky_slab, whole_of(test_matrix, PAIRS, 1), preferred_element_type=jnp.float32
    )
    sketch = total_of_pieces(partial_value, "aux")
    gram_matrix = total_of(gram_local(sketch), PAIRS, (0, 1))
    basis_full = basis_from(gram_matrix, sketch)
    return sum_by_axis(
        jnp.dot(
            basis_full,
            cholesky_slab,
            precision=lax.Precision.HIGHEST,
            preferred_element_type=jnp.float32,
        ),
        PAIRS,
    )


def solution(mesh):
    split = Mesh(mesh.devices.reshape(8, 4, mesh.shape["aux"]), ("pairs_0", "pairs_1", "aux"))
    return jax.shard_map(
        body,
        mesh=split,
        in_specs=(P(PAIRS, "aux"), P("aux", PAIRS)),
        out_specs=P(PAIRS, "aux"),
        check_vma=False,
    )
```

profile of v0, /device:TPU:8, one launch (start us, length us, event | category | flops | bytes accessed | tf_op | source)
XLA Modules:
  0.0 720.5 jit_solution(13642898595764134096)
XLA Ops:
  6.5 15.4 %all_gather.18 = bf16[4480,96]{0,1:T(8,128)(2,1)} all-gather(bf16[4480,24]{0,1:T(8,128)(2,1)} %param.3), channel_id=1, replica_groups=mesh['pairs_0'=8,'pairs_1'=4,'aux'=8] {'pairs_1'}, dimensions={1}, use_global_device_ids=true | all-gather | bytes 1075200 | tf_op jit(solution)/shard_map/all_gather | solution.py:12
  22.1 82.6 %all-gather.5.cloned.1.call-done = bf16[4480,768]{0,1:T(8,128)(2,1)} async-done(((bf16[4480,96]{0,1:T(8,128)(2,1)}), bf16[4480,768]{0,1:T(8,128)(2,1)}) %all-gather.5.cloned.1.call-update) | async-done | bytes 6881296 | tf_op jit(solution)/shard_map/all_gather | solution.py:12
  104.6 5.8 fusion.52
  110.6 42.1 %all-gather.9.cloned.1.call-done = f32[2048,768]{1,0:T(8,128)} async-done(((f32[256,768]{1,0:T(8,128)}), f32[2048,768]{1,0:T(8,128)}) %all-gather.9.cloned.1.call-update) | async-done | bytes 6291472 | tf_op jit(solution)/shard_map/all_gather | solution.py:17
  152.6 3.2 reduce_sum.9
  157.0 4.6 fusion.1
  161.7 43.5 %reduce-scatter.7.cloned.1.call-done = f32[4,24,768]{2,1,0:T(8,128)} async-done(((f32[32,24,768]{2,1,0:T(8,128)}), f32[4,24,768]{2,1,0:T(8,128)}) %reduce-scatter.7.cloned.1.call-update) | async-done | bytes 294928 | tf_op jit(solution)/shard_map/reduce_scatter | solution.py:32
  205.3 23.1 %reduce-scatter.9.cloned.1.call-done = f32[1,24,768]{2,1,0:T(8,128)} async-done(((f32[4,24,768]{2,1,0:T(8,128)}), f32[1,24,768]{2,1,0:T(8,128)}) %reduce-scatter.9.cloned.1.call-update) | async-done | bytes 73744 | tf_op jit(solution)/shard_map/reduce_scatter | solution.py:32
  228.4 13.9 %all_gather.22 = f32[4,24,768]{2,1,0:T(8,128)} all-gather(f32[1,24,768]{2,1,0:T(8,128)} %reduce-scatter.9.cloned.1.call-done), channel_id=1, replica_groups=mesh['pairs_0'=8,'pairs_1'=4,'aux'=8] {'pairs_1'}, dimensions={0}, use_global_device_ids=true | all-gather | bytes 368640 | tf_op jit(solution)/shard_map/all_gather | solution.py:39
  242.4 42.3 %all-gather.7.cloned.1.call-done = f32[32,24,768]{2,1,0:T(8,128)} async-done(((f32[4,24,768]{2,1,0:T(8,128)}), f32[32,24,768]{2,1,0:T(8,128)}) %all-gather.7.cloned.1.call-update) | async-done | bytes 2359312 | tf_op jit(solution)/shard_map/all_gather | solution.py:39
  284.7 3.5 copy.11
  292.2 11.7 %cholesky.165 = f32[128,128]{1,0:T(8,128)S(1)} custom-call(f32[128,128]{1,0:T(8,128)S(1)} %cholesky.424), custom_call_target="Cholesky" | custom-call | tf_op jit(solution)/shard_map/jit(cholesky)/cholesky | solution.py:70
  305.5 9.8 %custom-call.47 = f32[1,128,128]{1,2,0:T(8,128)S(1)} custom-call(f32[1,128,128]{2,1,0:T(8,128)S(1)} %get-tuple-element.48), custom_call_target="InvertDiagBlocksLowerTriangular" | custom-call | tf_op jit(solution)/shard_map/jit(cholesky)/cholesky | solution.py:70
  318.9 11.7 %cholesky.188 = f32[128,128]{1,0:T(8,128)S(1)} custom-call(f32[128,128]{1,0:T(8,128)S(1)} %cholesky.428), custom_call_target="Cholesky" | custom-call | tf_op jit(solution)/shard_map/jit(cholesky)/cholesky | solution.py:70
  331.3 10.0 %custom-call.48 = f32[1,128,128]{1,2,0:T(8,128)S(1)} custom-call(f32[1,128,128]{2,1,0:T(8,128)S(1)} %get-tuple-element.45), custom_call_target="InvertDiagBlocksLowerTriangular" | custom-call | tf_op jit(solution)/shard_map/jit(cholesky)/cholesky | solution.py:70
  344.1 11.7 %cholesky.354 = f32[128,128]{1,0:T(8,128)S(1)} custom-call(f32[128,128]{1,0:T(8,128)S(1)} %cholesky.433), custom_call_target="Cholesky" | custom-call | tf_op jit(solution)/shard_map/jit(cholesky)/cholesky | solution.py:70
  357.2 9.8 %custom-call.49 = f32[1,128,128]{1,2,0:T(8,128)S(1)} custom-call(f32[1,128,128]{2,1,0:T(8,128)S(1)} %get-tuple-element.42), custom_call_target="InvertDiagBlocksLowerTriangular" | custom-call | tf_op jit(solution)/shard_map/jit(cholesky)/cholesky | solution.py:70
  369.9 11.9 %cholesky.373 = f32[128,128]{1,0:T(8,128)S(1)} custom-call(f32[128,128]{1,0:T(8,128)S(1)} %cholesky.438), custom_call_target="Cholesky" | custom-call | tf_op jit(solution)/shard_map/jit(cholesky)/cholesky | solution.py:70
  383.1 9.8 %custom-call.50 = f32[1,128,128]{1,2,0:T(8,128)S(1)} custom-call(f32[1,128,128]{2,1,0:T(8,128)S(1)} %get-tuple-element.39), custom_call_target="InvertDiagBlocksLowerTriangular" | custom-call | tf_op jit(solution)/shard_map/jit(cholesky)/cholesky | solution.py:70
  395.6 11.7 %cholesky.392 = f32[128,128]{1,0:T(8,128)S(1)} custom-call(f32[128,128]{1,0:T(8,128)S(1)} %cholesky.443), custom_call_target="Cholesky" | custom-call | tf_op jit(solution)/shard_map/jit(cholesky)/cholesky | solution.py:70
  408.7 9.8 %custom-call.51 = f32[1,128,128]{1,2,0:T(8,128)S(1)} custom-call(f32[1,128,128]{2,1,0:T(8,128)S(1)} %get-tuple-element.36), custom_call_target="InvertDiagBlocksLowerTriangular" | custom-call | tf_op jit(solution)/shard_map/jit(cholesky)/cholesky | solution.py:70
  420.9 11.9 %cholesky.410 = f32[128,128]{1,0:T(8,128)S(1)} custom-call(f32[128,128]{1,0:T(8,128)S(1)} %convolution_subtract_fusion.9), custom_call_target="Cholesky" | custom-call | tf_op jit(solution)/shard_map/jit(cholesky)/cholesky | solution.py:70
  438.7 3.3 select_select_fusion
  442.0 20.4 %while.1 = (s32[]{:T(128)}, f32[768,768]{1,0:T(8,128)}, s32[6,2]{0,1:T(2,128)S(1)}, f32[6,128,128]{2,1,0:T(8,128)}, s32[]{:T(128)}) while((s32[]{:T(128)}, f32[768,768]{1,0:T(8,128)}, s32[6,2]{0,1:T(2,128)S(1)}, f32[6,128,128]{2,1,0:T(8,128)}, s32[]{:T(128)}) %tuple.40), condition=%wide.while_cond, body=%wide.while_body.sunk | while | flops 2 | bytes 132205 | solution.py:71
  442.6 2.8 bitcast_dynamic-update-slice_fusion.2
  446.0 2.8 bitcast_dynamic-update-slice_fusion.2
  449.4 2.8 bitcast_dynamic-update-slice_fusion.2
  452.9 2.8 bitcast_dynamic-update-slice_fusion.2
  462.4 59.8 %custom-call.52 = f32[6,128,128]{1,2,0:T(8,128)S(1)} custom-call(f32[6,128,128]{2,1,0:T(8,128)} %get-tuple-element.12), custom_call_target="InvertDiagBlocksLowerTriangular" | custom-call | tf_op jit(solution)/shard_map/jit(_solve_triangular)/triangular_solve | solution.py:71
  530.6 8.7 %fusion.53 = f32[768,4480]{1,0:T(8,128)} fusion(f32[768,256]{1,0:T(8,128)S(1)} %convolution_dynamic-update-slice_fusion.2, bf16[256,4480]{1,0:T(8,128)(2,1)S(1)} %copy-done), kind=kOutput, calls=%fused_computation.115 | convolution fusion | flops 10569646080 | bytes 16842752 | tf_op jit(solution)/shard_map/dot_general | solution.py:82
  539.4 144.5 %reduce-scatter.11.cloned.1.call-done = f32[96,4480]{1,0:T(8,128)} async-done(((f32[768,4480]{1,0:T(8,128)}), f32[96,4480]{1,0:T(8,128)}) %reduce-scatter.11.cloned.1.call-update) | async-done | bytes 1720336 | tf_op jit(solution)/shard_map/reduce_scatter | solution.py:56
  683.9 29.2 %reduce-scatter.13.cloned.1.call-done = f32[24,4480]{1,0:T(8,128)} async-done(((f32[96,4480]{1,0:T(8,128)}), f32[24,4480]{1,0:T(8,128)}) %reduce-scatter.13.cloned.1.call-update) | async-done | bytes 430096
  (77 shorter events, 45.7 us)
Async XLA Ops:
  6.5 98.1 %copy-start = (bf16[256,4480]{1,0:T(8,128)(2,1)S(1)}, bf16[256,4480]{1,0:T(8,128)(2,1)}, u32[]{:S(2)}) copy-start(bf16[256,4480]{1,0:T(8,128)(2,1)} %param.2) | copy-start | bytes 6881284
  6.5 98.1 %all-gather.5.cloned.1.call-start = ((), (), s32[]{:S(2)}) async-start(), calls=%async_computation.4 | async-start | bytes 7741440 | tf_op jit(solution)/shard_map/all_gather | solution.py:12
  22.0 130.6 %all-gather.9.cloned.1.call-start = ((), (), s32[]{:S(2)}) async-start(), calls=%async_computation.9 | async-start | bytes 7077888 | tf_op jit(solution)/shard_map/all_gather | solution.py:17
  110.5 94.7 %reduce-scatter.7.cloned.1.call-start = ((), (), s32[]{:S(2)}) async-start(), calls=%async_computation.5 | async-start | bytes 2654208 | tf_op jit(solution)/shard_map/reduce_scatter | solution.py:32
  161.7 66.7 %reduce-scatter.9.cloned.1.call-start = ((), (), s32[]{:S(2)}) async-start(), calls=%async_computation.6 | async-start | bytes 368640 | tf_op jit(solution)/shard_map/reduce_scatter | solution.py:32
  205.2 79.4 %all-gather.7.cloned.1.call-start = ((), (), s32[]{:S(2)}) async-start(), calls=%async_computation.7 | async-start | bytes 2654208 | tf_op jit(solution)/shard_map/all_gather | solution.py:39
  242.3 441.6 %reduce-scatter.11.cloned.1.call-start = ((), (), s32[]{:S(2)}) async-start(), calls=%async_computation.8 | async-start | bytes 15482880 | tf_op jit(solution)/shard_map/reduce_scatter | solution.py:56
  290.8 1.4 copy-start.2
  438.7 83.5 %copy-start.1 = (f32[256,768]{0,1:T(8,128)S(1)}, f32[256,768]{0,1:T(8,128)}, u32[]{:S(2)}) copy-start(f32[256,768]{0,1:T(8,128)} %copy.10) | copy-start | bytes 2359300
  539.4 173.8 %reduce-scatter.13.cloned.1.call-start = ((), (), s32[]{:S(2)}) async-start(), calls=%async_computation.10 | async-start | bytes 2150400
Sparse Core Ops, SparseCore 0:
  22.1 82.4 all-gather.4
  110.6 41.9 all-gather.8
  161.8 43.3 reduce-scatter.6
  207.6 20.7 reduce-scatter.8
  242.5 42.1 all-gather.6
  539.5 144.3 reduce-scatter.10
  686.5 26.6 reduce-scatter.12
where the time goes:
time: 727 us; the launch traced here: 720 us
  waiting for transfers between devices  407 us (56%)
  other arithmetic  196 us (27%)
  matrix products  41.8 us (6%)
  blocking collectives  29.4 us (4%)
  local copies, waits for them, and re-layouts  28 us (4%)
  between operations  18 us (2%)
    reduce_scatter x1, waiting for transfers between devices, sum_by_axis(): total = lax.psum_scatter(total, axis, scatter_dimension=0, tiled=True)  145 us
    another operation x22, other arithmetic, basis_from(): lower_factor = jnp.linalg.cholesky(gram_matrix)  127 us
    all_gather x1, waiting for transfers between devices, whole_of(): x = lax.all_gather(x, axis, axis=dim, tiled=True)  82.6 us
    reduce_scatter x2, waiting for transfers between devices, own_block(): blocks = lax.psum_scatter(blocks, axes[k], scatter_dimension=0, tiled=True)  66.6 us
    another operation x3, other arithmetic, basis_from(): jax.scipy.linalg.solve_triangular(lower_factor, sketch_part.T, lower=True)  63.1 us
    all_gather x1, waiting for transfers between devices, gather_in_order(): blocks = lax.all_gather(blocks, axes[k], axis=0, tiled=True)  42.3 us
    all_gather x1, waiting for transfers between devices, total_of_pieces(): return lax.all_gather(x, axis).sum(0)  42.1 us
    unnamed x8, waiting for transfers between devices  29.3 us
  transfers between devices with their start and end apart: 7, of which 7 were waited for; matrix products, arithmetic and copies ran while one was open for 0% of the time, Pallas kernels for 0%

commit v1 on v0

v1 whole, which is shorter than its diff:
```python
import functools
import jax, jax.numpy as jnp
from jax import lax
from jax.experimental import pallas as pl
from jax.experimental.pallas import tpu as pltpu
from jax.sharding import Mesh
from jax.sharding import PartitionSpec as P
HI = lax.Precision.HIGHEST
F32 = jnp.float32
B = 128

def dot(x, y, dims, precision=HI):
    return lax.dot_general(x, y, (dims, ((), ())), precision=precision, preferred_element_type=F32)
NN = ((1,), (0,)); NT = ((1,), (1,)); TN = ((0,), (0,))

def lanes(x, j): return jnp.broadcast_to(x[:, j:j + 1], (x.shape[0], 128))
def row(x, j): return jnp.broadcast_to(x[j:j + 1, :], (8, 128))

def factor_panels(m, v, lo, hi):
    sub = lax.broadcasted_iota(jnp.int32, (8, 128), 0)
    for t in range(lo, hi):
        k = 8 * t
        left, right = m[k:k + 8, :128], m[k:k + 8, 128:]
        cols = [lanes(left, k + j) for j in range(8)]
        d = {(i, j): row(cols[j], i) for i in range(8) for j in range(i + 1)}
        l, inv = {}, []
        for j in range(8):
            r = lax.rsqrt(d[j, j])
            inv.append(r)
            for i in range(j + 1, 8):
                l[i, j] = d[i, j] * r
            for i in range(j + 1, 8):
                for h in range(j + 1, i + 1):
                    d[i, h] = d[i, h] - l[i, j] * l[h, j]
        rows = []
        for part in (left, right):
            raw = [row(part, i) for i in range(8)]
            done = []
            for i in range(8):
                x = raw[i]
                for j in range(i):
                    x = x - l[i, j] * done[j]
                done.append(x * inv[i])
            rows.append(done)
        tile = rows[1][0]
        for i in range(1, 8):
            tile = jnp.where(sub == i, rows[1][i], tile)
        v[k:k + 8, :] = tile
        if t < 15:
            q = []
            for done in rows:
                back = [None] * 8
                for i in reversed(range(8)):
                    x = done[i]
                    for j in range(i + 1, 8):
                        x = x - l[j, i] * back[j]
                    back[i] = x * inv[i]
                q.append(back)
            e = k + 8
            ml, mr = m[e:, :128], m[e:, 128:]
            al, ar = ml, mr
            for i in range(8):
                c = jnp.broadcast_to(ml[:, k + i:k + i + 1], ml.shape)
                al = al - c * q[0][i][:1, :]
                ar = ar - c * q[1][i][:1, :]
            m[e:, :128] = al
            m[e:, 128:] = ar

def chol_block(a, w, lfac, m, v, b, n=6):
    s, e = b * B, (b + 1) * B
    vb = v[...]
    w[s:e, s:e] = vb
    if b:
        part = dot(lfac[s:e, :s], w[:s, :s], NN)
        w[s:e, :s] = -dot(vb, part, NN)
    if b < n - 1:
        lfac[e:, s:e] = dot(a[e:, s:e], vb, NT)
        for j in range(b + 1, n):
            js, je = j * B, (j + 1) * B
            a[js:, js:je] = a[js:, js:je] - dot(lfac[js:, s:e], lfac[js:je, s:e], NT)

MESH = pl.DeviceIdType.MESH
NZ, NY, NX = 8, 4, 4
AXES = ("z", "y", "x", "c")
SIZES = {"z": NZ, "y": NY, "x": NX, "c": 2}
VM = pl.BlockSpec(memory_space=pltpu.VMEM)
ANY = pl.BlockSpec(memory_space=pl.ANY)
DMA = pltpu.SemaphoreType.DMA


def step_to(axis, hops):
    return lax.rem(lax.axis_index(axis) + hops, SIZES[axis])


def greet(peers):
    barrier = pltpu.get_barrier_semaphore()
    for axis, hops in peers:
        pl.semaphore_signal(barrier, inc=1, device_id={axis: step_to(axis, hops)}, device_id_type=MESH)
    pl.semaphore_wait(barrier, len(peers))


def send(src, dst, sems, k, axis, hops):
    copy = pltpu.make_async_remote_copy(
        src_ref=src, dst_ref=dst, send_sem=sems[0].at[k], recv_sem=sems[1].at[k],
        device_id={axis: step_to(axis, hops)}, device_id_type=MESH,
    )
    copy.start()
    return copy


def ring_gather(block, own, axis, cuts, sems, base):
    n = SIZES[axis]
    me = lax.axis_index(axis)
    lo, mid, hi = cuts
    far = n // 2
    copies = []
    for s in range(far):
        last = s == far - 1
        pair = []
        for k, way in enumerate((1, n - 1)):
            if last:
                a, b = (lo, mid) if k == 0 else (mid, hi)
            else:
                a, b = lo, hi
            who = lax.rem(me + (n - s if k == 0 else s), n)
            src = own(a, b) if s == 0 else block(who, a, b)
            pair.append(send(src, block(who, a, b), sems, base + 2 * s + k, axis, way))
        copies += pair
        yield copies
        for c in pair:
            c.wait_recv()


def gather_kernel(t, g, send_sems, recv_sems, own_sem):
    z, y = lax.axis_index("z"), lax.axis_index("y")
    K = t.shape[1]
    sems = (send_sems, recv_sems)
    cut = 14 * 128
    keep = pltpu.make_async_copy(t, g.at[z, y], own_sem)
    keep.start()
    greet([("y", 1), ("y", NY - 1), ("z", 1), ("z", NZ - 1)])
    own = lambda a, b: t.at[:, a:b]
    lcuts, rcuts = (0, 7 * 128, cut), (cut, cut + 11 * 128, K)
    ly = ring_gather(lambda i, a, b: g.at[z, i, :, a:b], own, "y", lcuts, sems, 0)
    rz = ring_gather(lambda i, a, b: g.at[i, y, :, a:b], own, "z", rcuts, sems, 4)
    lz = ring_gather(lambda i, a, b: g.at[i, :, :, a:b], lambda a, b: g.at[z, :, :, a:b], "z", lcuts, sems, 12)
    ry = ring_gather(lambda i, a, b: g.at[:, i, :, a:b], lambda a, b: g.at[:, y, :, a:b], "y", rcuts, sems, 20)
    done = []
    def go(gen, times=1):
        for _ in range(times):
            try:
                held = next(gen)
                if not any(h is held for h in done):
                    done.append(held)
            except StopIteration:
                return
    go(ly); go(rz); go(ly); go(rz); go(ly)
    keep.wait()
    go(lz); go(rz); go(rz); go(rz); go(ry)
    go(lz); go(lz); go(ry); go(lz); go(lz); go(ry)
    for held in done:
        for c in held:
            c.wait_send()


def gather(t):
    d, K = t.shape
    g = pl.pallas_call(
        gather_kernel, out_shape=jax.ShapeDtypeStruct((NZ, NY, d, K), t.dtype),
        in_specs=[ANY], out_specs=ANY,
        scratch_shapes=[DMA((24,)), DMA((24,)), DMA],
        compiler_params=pltpu.CompilerParams(collective_id=0, has_side_effects=True), name="gather",
    )(t)
    return g.reshape(NZ * NY * d, K)


def total_kernel(part, out, near, acc, far, send_sems, recv_sems):
    x, c = lax.axis_index("x"), lax.axis_index("c")
    R = part.shape[0]
    h, q = R // 2, R // 8
    sems = (send_sems, recv_sems)
    greet([("c", 1)] + [("x", i) for i in (1, 2, 3)])
    mine = pl.multiple_of(c * h, h)
    other = pl.multiple_of((1 - c) * h, h)
    first = send(part.at[pl.ds(other, h)], near, sems, 0, "c", 1)
    first.wait_recv()
    acc[...] = part[pl.ds(mine, h), :] + near[...]
    spread = []
    for i in (1, 2, 3):
        o = pl.multiple_of(step_to("x", i) * q, q)
        spread.append(send(acc.at[pl.ds(o, q)], far.at[i - 1], sems, i, "x", i))
    o = pl.multiple_of(x * q, q)
    total = acc[pl.ds(o, q), :]
    for i in (1, 2, 3):
        spread[i - 1].wait_recv()
        total = total + far[i - 1]
    own = pl.ds(pl.multiple_of(mine + o, q), q)
    out[own, :] = total
    back = [send(out.at[own], out.at[own], sems, 3 + i, "x", i) for i in (1, 2, 3)]
    for b in back:
        b.wait_recv()
    half = out.at[pl.ds(mine, h)]
    last = send(half, half, sems, 7, "c", 1)
    last.wait_recv()
    for copy in (first, *spread, *back, last):
        copy.wait_send()


def total_over_aux(part):
    R, C = part.shape
    return pl.pallas_call(
        total_kernel, out_shape=jax.ShapeDtypeStruct((R, C), F32),
        in_specs=[VM], out_specs=VM,
        scratch_shapes=[pltpu.VMEM((R // 2, C), F32), pltpu.VMEM((R // 2, C), F32), pltpu.VMEM((3, R // 8, C), F32), DMA((8,)), DMA((8,))],
        compiler_params=pltpu.CompilerParams(collective_id=1, has_side_effects=True), name="total",
    )(part)


SLOTS = 3


def place(t):
    at_least = lambda k: (t + 32 - k) // 32
    i = at_least(1) + at_least(3) + at_least(6) + at_least(10) + at_least(15)
    j = t - i * (i + 1) // 2
    spare = at_least(21)
    return i, j * (1 - spare)


def gram_compute(s, gp):
    a = lax.axis_index("x") * 2 + lax.axis_index("c")
    for k in range(SLOTS):
        i, j = place(a * SLOTS + k)
        li = s[:, pl.ds(pl.multiple_of(i * B, B), B)]
        lj = s[:, pl.ds(pl.multiple_of(j * B, B), B)]
        gp[k * B:(k + 1) * B, :] = dot(li, lj, TN)


GRAM_PEERS = [("z", i) for i in range(1, NZ)] + [("y", i) for i in range(1, NY)] + [("x", i) for i in range(1, NX)] + [("c", 1)]
GRAM_COPIES = 7 + 3 + 7 + 3 + 1


def gram_exchange(gp, gz, own, gy, full, sems, base):
    x, c, z = lax.axis_index("x"), lax.axis_index("c"), lax.axis_index("z")
    q = gp.shape[0] // NZ
    copies = []
    ones = []
    for i in range(1, NZ):
        o = pl.multiple_of(step_to("z", i) * q, q)
        ones.append(send(gp.at[pl.ds(o, q)], gz.at[i - 1], sems, base + i - 1, "z", i))
    yield
    mine = pl.ds(pl.multiple_of(z * q, q), q)
    total = gp[mine, :]
    for i in range(1, NZ):
        ones[i - 1].wait_recv()
        total = total + gz[i - 1]
    own[...] = total
    twos = [send(own, gy.at[i - 1], sems, base + 6 + i, "y", i) for i in range(1, NY)]
    yield
    total = own[...]
    for i in range(1, NY):
        twos[i - 1].wait_recv()
        total = total + gy[i - 1]
    full[x, c, mine, :] = total
    here = full.at[x, c, mine]
    threes = [send(here, here, sems, base + 9 + i, "z", i) for i in range(1, NZ)]
    yield
    for t in threes:
        t.wait_recv()
    all_mine = full.at[x, c]
    fours = [send(all_mine, all_mine, sems, base + 16 + i, "x", i) for i in range(1, NX)]
    yield
    for t in fours:
        t.wait_recv()
    column = full.at[:, c]
    five = send(column, column, sems, base + 20, "c", 1)
    yield
    five.wait_recv()
    for t in (*ones, *twos, *threes, *fours, five):
        t.wait_send()


GRAM_SCRATCH = [pltpu.VMEM((SLOTS * B, B), F32), pltpu.VMEM((NZ - 1, SLOTS * B // NZ, B), F32), pltpu.VMEM((SLOTS * B // NZ, B), F32), pltpu.VMEM((NY - 1, SLOTS * B // NZ, B), F32)]


HALF = 384


class Stream:
    def __init__(self, axis, way, local, buf, sink, sems, base):
        self.axis, self.way, self.n = axis, way, SIZES[axis]
        self.local, self.buf, self.sink, self.sems, self.base = local, buf, sink, sems, base

    def block(self, back):
        n = self.n
        return lax.rem(lax.axis_index(self.axis) + (2 * n - back if self.way == 1 else back), n)

    def copy(self, s):
        return pltpu.make_async_remote_copy(
            src_ref=self.local(self.block(1)) if s == 0 else self.buf.at[s - 1],
            dst_ref=self.buf.at[s],
            send_sem=self.sems[0].at[self.base + s], recv_sem=self.sems[1].at[self.base + s],
            device_id={self.axis: step_to(self.axis, 1 if self.way == 1 else self.n - 1)}, device_id_type=MESH,
        )

    def serve(self, s):
        self.copy(s).wait_recv()
        total = self.buf[s] + self.local(self.block(2 + s))[...]
        if s < self.n - 2:
            self.buf[s] = total
            self.copy(s + 1).start()
        else:
            self.sink[...] = total

    def finish(self):
        for s in range(self.n - 1):
            self.copy(s).wait_send()


def sub_start(i):
    return pl.multiple_of(i * 140 // 8 * 8, 8)


Z_ROWS = ((1, 0, 144), (1, 144, 136), (-1, 280, 144), (-1, 424, 136))
Y_ROWS = ((1, 0, 40), (1, 40, 32), (-1, 72, 40), (-1, 112, 32))
ZY_ROWS = ((1, 0, 72), (-1, 72, 72))
RS_COPIES = 4 * 7 + 4 * 3 + 2 * 3 + 4 * 7


def finish_kernel(slab, s, out, w, c, resz, resy, *rest):
    zb, yb, zyb, yzb = rest[0:4], rest[4:8], rest[8:10], rest[10:14]
    hi, lo, gp, gz, own, gy, full, a, lfac, m, v, ss, rs, gs, gr = rest[14:]
    sems = (ss, rs)
    tiles = slab.shape[1] // B
    greet(GRAM_PEERS)
    exchange = gram_exchange(gp, gz, own, gy, full, (gs, gr), 0)
    gram_compute(s, gp)
    next(exchange)
    hi[...] = s[...].astype(jnp.bfloat16)
    lo[...] = (s[...] - hi[...].astype(F32)).astype(jnp.bfloat16)

    def tile(t, _):
        part = slab[:, pl.ds(pl.multiple_of(t * B, B), B)]
        value = lax.dot_general(part, hi[...], (TN, ((), ())), preferred_element_type=F32)
        value = value + lax.dot_general(part, lo[...], (TN, ((), ())), preferred_element_type=F32)
        for k in range(8):
            q = t * 8 + k
            c[q // 35, pl.ds(pl.multiple_of(lax.rem(q, 35) * 16, 16), 16), :] = value[k * 16:(k + 1) * 16, :]
        return 0

    lax.fori_loop(0, 20, tile, 0)
    next(exchange)
    lax.fori_loop(20, tiles, tile, 0)
    next(exchange)

    base = 0
    zs, ys, zys, yzs = [], [], [], []
    for k, (way, o, n) in enumerate(Z_ROWS):
        local = lambda i, o=o, n=n: c.at[i, o:o + n, 0:HALF]
        zs.append(Stream("z", way, local, zb[k], resz.at[o:o + n], sems, base))
        base += NZ - 1
    for k, (way, o, n) in enumerate(Y_ROWS):
        local = lambda i, o=o, n=n: c.at[:, pl.ds(sub_start(i) + o, n), HALF:2 * HALF]
        ys.append(Stream("y", way, local, yb[k], resy.at[:, o:o + n], sems, base))
        base += NY - 1
    for k, (way, o, n) in enumerate(ZY_ROWS):
        local = lambda i, o=o, n=n: resz.at[pl.ds(sub_start(i) + o, n)]
        zys.append(Stream("y", way, local, zyb[k], out.at[o:o + n, 0:HALF], sems, base))
        base += NY - 1
    for k, (way, o, n) in enumerate(Y_ROWS):
        local = lambda i, o=o, n=n: resy.at[i, o:o + n]
        yzs.append(Stream("z", way, local, yzb[k], out.at[o:o + n, HALF:2 * HALF], sems, base))
        base += NZ - 1
    for k in (0, 2, 1, 3):
        zs[k].copy(0).start()
        ys[k].copy(0).start()

    events = []
    def later(when, action):
        events.append((when, len(events), action))
    for step in range(NZ - 1):
        for k in (0, 2, 1, 3):
            later(9.3 * (step + 1) + (1.7 if k % 2 else -2.9), lambda k=k, step=step: zs[k].serve(step))
    for step in range(NY - 1):
        for k in (0, 2, 1, 3):
            later(19 * (step + 1) + (1.7 if k % 2 else -6.8), lambda k=k, step=step: ys[k].serve(step))
    later(67, lambda: [x.copy(0).start() for x in zys])
    later(58.8, lambda: [yzs[k].copy(0).start() for k in (0, 2, 1, 3)])
    for step in range(NY - 1):
        for k in (0, 1):
            later(71 + 4 * step, lambda k=k, step=step: zys[k].serve(step))
    for step in range(NZ - 1):
        for k in (0, 2, 1, 3):
            later(62.5 + 3.3 * step, lambda k=k, step=step: yzs[k].serve(step))
    events.sort(key=lambda e: e[:2])

    def due(now):
        ready = []
        while events and events[0][0] <= now:
            ready.append(events.pop(0)[2])
        return ready

    next(exchange)
    now = 8
    for cost in (10, 4):
        for action in due(now):
            action()
        now += cost
        try:
            next(exchange)
        except StopIteration:
            pass
    for action in due(now):
        action()
    for _ in exchange:
        pass
    n = 6
    for i in range(n):
        for j in range(i + 1):
            t = i * (i + 1) // 2 + j
            a[i * B:(i + 1) * B, j * B:(j + 1) * B] = full[t // 6, t // 3 % 2, (t % 3) * B:(t % 3 + 1) * B, :]
    w[...] = jnp.zeros_like(w)
    row_of = lax.broadcasted_iota(jnp.int32, (B, B), 0)
    col_of = lax.broadcasted_iota(jnp.int32, (B, B), 1)
    eye = jnp.where(row_of == col_of, 1.0, 0.0).astype(F32)
    table = {}
    for b in range(n):
        for piece in range(4):
            now += 1.35
            table[b, piece] = due(now)
            now += 0.3 * len(table[b, piece])
        now += 2

    def step(b, _):
        o = pl.multiple_of(b * B, B)
        m[:, :B] = a[pl.ds(o, B), pl.ds(o, B)]
        m[:, B:] = eye
        for piece in range(4):
            factor_panels(m, v, 4 * piece, 4 * piece + 4)
            for k in range(n):
                if table[k, piece]:
                    @pl.when(b == k)
                    def _():
                        for action in table[k, piece]:
                            action()
        for k in range(n):
            @pl.when(b == k)
            def _():
                chol_block(a, w, lfac, m, v, k)
        return 0

    lax.fori_loop(0, n, step, 0)
    for action in due(1e9):
        action()
    for stream in (*zs, *ys, *zys, *yzs):
        stream.finish()


def finish(slab, s):
    bf = jnp.bfloat16
    R, C = s.shape
    vm = lambda *shape: pltpu.VMEM(shape, F32)
    return pl.pallas_call(
        finish_kernel,
        out_shape=(jax.ShapeDtypeStruct((144, C), F32), jax.ShapeDtypeStruct((C, C), F32)),
        in_specs=[VM, VM], out_specs=(VM, VM),
        scratch_shapes=[
            vm(NZ, 560, C), vm(560, HALF), vm(NZ, 144, HALF),
            *[vm(NZ - 1, n, HALF) for _, _, n in Z_ROWS],
            *[vm(NY - 1, NZ, n, HALF) for _, _, n in Y_ROWS],
            *[vm(NY - 1, n, HALF) for _, _, n in ZY_ROWS],
            *[vm(NZ - 1, n, HALF) for _, _, n in Y_ROWS],
            pltpu.VMEM((R, C), bf), pltpu.VMEM((R, C), bf),
            *GRAM_SCRATCH, vm(NX, 2, SLOTS * B, B), vm(C, C), vm(C, C), vm(B, 2 * B), vm(B, B),
            DMA((RS_COPIES,)), DMA((RS_COPIES,)), DMA((GRAM_COPIES,)), DMA((GRAM_COPIES,)),
        ],
        compiler_params=pltpu.CompilerParams(collective_id=2, has_side_effects=True, vmem_limit_bytes=60 * 2**20), name="finish",
    )(slab, s)


def body(slab, test):
    tests = gather(test.T)
    part = lax.dot_general(slab, tests, (NT, ((), ())), preferred_element_type=F32)
    sketch = total_over_aux(part)
    c, w = finish(slab, sketch)
    y = lax.axis_index("y")
    c = lax.dynamic_slice_in_dim(c, y * 140 % 8, 140, 0)
    p = lax.dot_general(w, c, (NT, ((), ())), precision=HI, preferred_element_type=F32)
    p = lax.all_to_all(p.reshape(NZ * NY, 24, -1), ("z", "y"), 0, 0, tiled=True)
    return p.transpose(1, 0, 2).reshape(24, -1)


def solution(mesh):
    split = Mesh(mesh.devices.reshape(NZ, NY, NX, 2), AXES)
    return jax.shard_map(
        body, mesh=split, in_specs=(P(("z", "y"), ("x", "c")), P(("x", "c"), ("z", "y"))),
        out_specs=P(("z", "y"), ("x", "c")), check_vma=False,
    )
```

time: 727 us -> 241 us (0.33)
  waiting for transfers between devices: 407 us -> 0 us
  Pallas kernels: 0 us -> 205 us
  other arithmetic: 196 us -> 0 us
  matrix products: 41.8 us -> 9.59 us
  local copies, waits for them, and re-layouts: 28 us -> 1.4 us
  between operations: 18 us -> 0.06 us
    reduce_scatter x3 -> x0, waiting for transfers between devices: 211 us -> none  [the longest x1 145 us: sum_by_axis(): total = lax.psum_scatter(total, axis, scatter_dimension=0, tiled=True)]
    pallas_call x0 -> x3, Pallas kernels: none -> 205 us  [the longest x1 119 us: finish(): pl.pallas_call(finish_kernel, out_shape=(jax.ShapeDtypeStruct((144, C), F...]
    another operation x25 -> x0, other arithmetic: 190 us -> none  [the longest x22 127 us: basis_from(): lower_factor = jnp.linalg.cholesky(gram_matrix)]
    all_gather x3 -> x0, waiting for transfers between devices: 167 us -> none  [the longest x1 82.6 us: whole_of(): x = lax.all_gather(x, axis, axis=dim, tiled=True)]
    all_gather x2 -> x0, blocking collectives: 29.4 us -> none  [the longest x1 15.4 us: whole_of(): x = lax.all_gather(x, axis, axis=dim, tiled=True)]
    unnamed x8 -> x0, waiting for transfers between devices: 29.3 us -> none
    another operation x26 -> x0, local copies, waits for them, and re-layouts: 25.5 us -> none
    all_to_all x0 -> x1, blocking collectives: none -> 24.7 us  [body(): p = lax.all_to_all(p.reshape(NZ * NY, 24, -1), ('z', 'y'), 0, 0, tiled=True)]
  transfers between devices with their start and end apart: 7 -> 0, of which waited for: 7 -> 0; matrix products, arithmetic and copies ran while one was open for 0% -> 0% of each run, Pallas kernels for 0% -> 0%
where the time goes in v1:
time: 241 us; the launch traced here: 240 us
  Pallas kernels  205 us (85%)
  blocking collectives  24.7 us (10%)
  matrix products  9.59 us (4%)
    pallas_call x1, Pallas kernels, finish(): pl.pallas_call(finish_kernel, out_shape=(jax.ShapeDtypeStruct((144, C), F...  119 us
    pallas_call x1, Pallas kernels, gather(): pl.pallas_call(gather_kernel, out_shape=jax.ShapeDtypeStruct((NZ, NY, d,...  64.8 us
    all_to_all x1, blocking collectives, body(): p = lax.all_to_all(p.reshape(NZ * NY, 24, -1), ('z', 'y'), 0, 0, tiled=True)  24.7 us
    pallas_call x1, Pallas kernels, total_over_aux(): pl.pallas_call(total_kernel, out_shape=jax.ShapeDtypeStruct((R, C), F32),...  20.5 us
    dot_general x1, matrix products, body(): lax.dot_general(slab, tests, (NT, ((), ())), preferred_element_type=F32)  5.86 us

profile of v1, /device:TPU:8, one launch (start us, length us, event | category | flops | bytes accessed | tf_op | source)
XLA Modules:
  0.0 240.4 jit_solution(18228838536565756883)
XLA Ops:
  0.0 0.0 copy-start
  0.0 64.8 %gather.1 = bf16[8,4,24,4480]{3,2,1,0:T(8,128)(2,1)} custom-call(bf16[24,4480]{1,0:T(8,128)(2,1)} %bitcast.10), custom_call_target="tpu_custom_call" | custom-call | tf_op jit(solution)/shard_map/gather/pallas_call | solution.py:168
  64.8 0.0 copy-done
  64.8 5.9 %fusion.3.part = f32[256,768]{1,0:T(8,128)} fusion(bf16[256,4480]{1,0:T(8,128)(2,1)S(1)} %copy-done, bf16[768,4480]{1,0:T(8,128)(2,1)} %bitcast.7), kind=kOutput, calls=%fused_computation.3 | convolution fusion | flops 1761607680 | bytes 9961472 | tf_op jit(solution)/shard_map/dot_general | solution.py:483
  70.7 20.5 %total.1.s = f32[256,768]{1,0:T(8,128)} custom-call(f32[256,768]{1,0:T(8,128)} %fusion.3.part), custom_call_target="tpu_custom_call" | custom-call | tf_op jit(solution)/shard_map/total/pallas_call | solution.py:211
  91.2 119.4 %finish.1 = (f32[144,768]{1,0:T(8,128)}, f32[768,768]{1,0:T(8,128)}) custom-call(bf16[256,4480]{1,0:T(8,128)(2,1)} %slab.1, f32[256,768]{1,0:T(8,128)} %total.1.s), custom_call_target="tpu_custom_call" | custom-call | tf_op jit(solution)/shard_map/finish/pallas_call | solution.py:463
  210.6 3.7 %fusion = f32[768,140]{1,0:T(8,128)S(1)} fusion(f32[768,768]{1,0:T(8,128)} %get-tuple-element.7, f32[144,768]{1,0:T(8,128)} %get-tuple-element.8, s32[]{:T(128)S(6)} %select_n.11), kind=kOutput, calls=%fused_computation | convolution fusion | flops 990904320 | bytes 3231748 | tf_op jit(solution)/shard_map/dot_general | solution.py:488
  214.3 24.7 %all_to_all.5 = f32[32,24,140]{2,1,0:T(8,128)S(1)} all-to-all(f32[32,24,140]{2,1,0:T(8,128)S(1)} %bitcast.9), channel_id=1, replica_groups=mesh['z'=8,'y'=4,'x'=4,'c'=2] {'z','y'}, dimensions={0} | all-to-all | bytes 860160 | tf_op jit(solution)/shard_map/all_to_all | solution.py:489
  239.0 0.3 copy.6
  239.3 1.1 reshape.11
Async XLA Ops:
  0.0 64.8 %copy-start = (bf16[256,4480]{1,0:T(8,128)(2,1)S(1)}, bf16[256,4480]{1,0:T(8,128)(2,1)}, u32[]{:S(2)}) copy-start(bf16[256,4480]{1,0:T(8,128)(2,1)} %slab.1) | copy-start | bytes 6881284

commit v2 on v1

--- a/solution.py
+++ b/solution.py
@@ -1,4 +1,5 @@
 import functools
+import heapq
 import jax, jax.numpy as jnp
 from jax import lax
 from jax.experimental import pallas as pl
@@ -108,67 +109,81 @@
     return copy
 
 
-def ring_gather(block, own, axis, cuts, sems, base):
-    n = SIZES[axis]
-    me = lax.axis_index(axis)
-    lo, mid, hi = cuts
-    far = n // 2
-    copies = []
-    for s in range(far):
-        last = s == far - 1
-        pair = []
-        for k, way in enumerate((1, n - 1)):
-            if last:
-                a, b = (lo, mid) if k == 0 else (mid, hi)
-            else:
-                a, b = lo, hi
-            who = lax.rem(me + (n - s if k == 0 else s), n)
-            src = own(a, b) if s == 0 else block(who, a, b)
-            pair.append(send(src, block(who, a, b), sems, base + 2 * s + k, axis, way))
-        copies += pair
-        yield copies
-        for c in pair:
-            c.wait_recv()
-
-
-def gather_kernel(t, g, send_sems, recv_sems, own_sem):
+RATE, HOP = 42e3, 2.0
+
+
+def gather_plan(d, cut, K):
+    free, heap, plan, count = {}, [], [], 0
+
+    def start(now, phase, way, step, dz, dy, lo, hi):
+        nonlocal count
+        axis = phase[1]
+        begin = max(now, free.get((axis, way), 0.0))
+        end = begin + d * (hi - lo) * 2 / RATE
+        free[axis, way] = end
+        job = (phase, axis, way, step, dz, dy, lo, hi, count)
+        count += 1
+        heapq.heappush(heap, (end + HOP, count, job))
+        return job
+
+    def both(now, phase, dz, dy, lo, hi):
+        return [start(now, phase, way, 0, dz, dy, lo, hi) for way in (1, -1)]
+
+    first = both(0, "ly", 0, 0, 0, cut) + both(0, "rz", 0, 0, cut, K)
+    first += both(0, "lz", 0, 0, 0, cut) + both(0, "ry", 0, 0, cut, K)
+    plan.append((None, first))
+    now = 0.0
+    while heap:
+        when, _, job = heapq.heappop(heap)
+        now = max(now, when) + 0.05
+        phase, axis, way, step, dz, dy, lo, hi, _ = job
+        dz, dy = (dz - way, dy) if axis == "z" else (dz, dy - way)
+        mid = lo + ((hi - lo) // 128 + 1) // 2 * 128
+        far = SIZES[axis] // 2
+        new = []
+        if step < far - 1:
+            a, b = (lo, hi) if step < far - 2 else ((lo, mid) if way == 1 else (mid, hi))
+            if b > a:
+                new.append(start(now, phase, way, step + 1, dz, dy, a, b))
+        if phase in ("ly", "rz"):
+            new += both(now, "lz" if phase == "ly" else "ry", dz, dy, lo, hi)
+        plan.append((job, new))
+    return plan, count, now
+
+
+def gather_kernel(plan, t, g, send_sems, recv_sems, own_sem):
     z, y = lax.axis_index("z"), lax.axis_index("y")
-    K = t.shape[1]
-    sems = (send_sems, recv_sems)
-    cut = 14 * 128
-    keep = pltpu.make_async_copy(t, g.at[z, y], own_sem)
-    keep.start()
+
+    def copy(job):
+        phase, axis, way, step, dz, dy, lo, hi, k = job
+        place = g.at[lax.rem(z + dz + NZ, NZ), lax.rem(y + dy + NY, NY), :, lo:hi]
+        return pltpu.make_async_remote_copy(
+            src_ref=t.at[:, lo:hi] if dz == dy == 0 else place, dst_ref=place,
+            send_sem=send_sems.at[k], recv_sem=recv_sems.at[k],
+            device_id={axis: step_to(axis, 1 if way == 1 else SIZES[axis] - 1)}, device_id_type=MESH,
+        )
+
     greet([("y", 1), ("y", NY - 1), ("z", 1), ("z", NZ - 1)])
-    own = lambda a, b: t.at[:, a:b]
-    lcuts, rcuts = (0, 7 * 128, cut), (cut, cut + 11 * 128, K)
-    ly = ring_gather(lambda i, a, b: g.at[z, i, :, a:b], own, "y", lcuts, sems, 0)
-    rz = ring_gather(lambda i, a, b: g.at[i, y, :, a:b], own, "z", rcuts, sems, 4)
-    lz = ring_gather(lambda i, a, b: g.at[i, :, :, a:b], lambda a, b: g.at[z, :, :, a:b], "z", lcuts, sems, 12)
-    ry = ring_gather(lambda i, a, b: g.at[:, i, :, a:b], lambda a, b: g.at[:, y, :, a:b], "y", rcuts, sems, 20)
-    done = []
-    def go(gen, times=1):
-        for _ in range(times):
-            try:
-                held = next(gen)
-                if not any(h is held for h in done):
-                    done.append(held)
-            except StopIteration:
-                return
-    go(ly); go(rz); go(ly); go(rz); go(ly)
+    for job, new in plan:
+        if job is not None:
+            copy(job).wait_recv()
+        for other in new:
+            copy(other).start()
+        if job is None:
+            keep = pltpu.make_async_copy(t, g.at[z, y], own_sem)
+            keep.start()
     keep.wait()
-    go(lz); go(rz); go(rz); go(rz); go(ry)
-    go(lz); go(lz); go(ry); go(lz); go(lz); go(ry)
-    for held in done:
-        for c in held:
-            c.wait_send()
+    for job, _ in plan[1:]:
+        copy(job).wait_send()
 
 
 def gather(t):
     d, K = t.shape
+    plan, count, _ = gather_plan(d, K // 128 * 2 // 5 * 128, K)
     g = pl.pallas_call(
-        gather_kernel, out_shape=jax.ShapeDtypeStruct((NZ, NY, d, K), t.dtype),
+        functools.partial(gather_kernel, plan), out_shape=jax.ShapeDtypeStruct((NZ, NY, d, K), t.dtype),
         in_specs=[ANY], out_specs=ANY,
-        scratch_shapes=[DMA((24,)), DMA((24,)), DMA],
+        scratch_shapes=[DMA((count,)), DMA((count,)), DMA],
         compiler_params=pltpu.CompilerParams(collective_id=0, has_side_effects=True), name="gather",
     )(t)
     return g.reshape(NZ * NY * d, K)
@@ -283,7 +298,98 @@
 GRAM_SCRATCH = [pltpu.VMEM((SLOTS * B, B), F32), pltpu.VMEM((NZ - 1, SLOTS * B // NZ, B), F32), pltpu.VMEM((SLOTS * B // NZ, B), F32), pltpu.VMEM((NY - 1, SLOTS * B // NZ, B), F32)]
 
 
+Z_ROWS = ((1, 0, 144), (1, 144, 136), (-1, 280, 144), (-1, 424, 136))
+Y_ROWS = ((1, 0, 40), (1, 40, 32), (-1, 72, 40), (-1, 112, 32))
+ZY_ROWS = ((1, 0, 72), (-1, 72, 72))
 HALF = 384
+KINDS = (("z", "z", Z_ROWS), ("y", "y", Y_ROWS), ("zy", "y", ZY_ROWS), ("yz", "z", Y_ROWS))
+
+
+def stream_specs():
+    specs = []
+    for kind, axis, rows in KINDS:
+        for k, (way, o, n) in enumerate(rows):
+            after = {"zy": tuple(("z", i) for i in range(4)), "yz": (("y", k),)}.get(kind, ())
+            specs.append(((kind, k), axis, way, n * HALF * 4 * (NZ if kind == "y" else 1), after))
+    return specs
+
+
+def finish_plan():
+    specs = {s[0]: s for s in stream_specs()}
+    free, heap, plan, count, ended = {}, [], [], 0, set()
+
+    def wire(now, axis, way, size):
+        end = max(now, free.get((axis, way), 0.0)) + size / RATE
+        free[axis, way] = end
+        return end + HOP
+
+    def post(when, what):
+        nonlocal count
+        count += 1
+        heapq.heappush(heap, (when, count, what))
+
+    def begin(now, name):
+        _, axis, way, size, _ = specs[name]
+        post(wire(now, axis, way, size), ("serve", name, 0))
+
+    def gram_sends(now, stage):
+        q = SLOTS * B * B * 4 // NZ
+        if stage in (0, 2):
+            when = max(wire(now, "z", way, 8 * q) for way in (1, -1)) + 1.5 * HOP
+        elif stage == 1:
+            when = max(wire(now, "y", way, 2 * q) for way in (1, -1)) + HOP
+        else:
+            when = now + (11.0 if stage == 3 else 3.5)
+        post(when, ("gram", stage + 1))
+
+    now = 1.5
+    gram_sends(now, 0)
+    now += 3.0
+    zfirst = [n for n, s in specs.items() if not s[4] and s[1] == "z"]
+    yfirst = [n for n, s in specs.items() if not s[4] and s[1] == "y"]
+    early = zfirst[0:3:2]
+    held = {1: yfirst, 2: [n for n in zfirst if n not in early]}
+
+    def launch(names):
+        for name in names:
+            begin(now, name)
+        plan.append(("begin", names))
+
+    launch(early)
+    plan.append(("tiles",))
+    now += 3.4
+    chol = []
+    while heap or chol:
+        if heap and (heap[0][0] <= now or not chol):
+            when, _, what = heapq.heappop(heap)
+            now = max(now, when)
+            plan.append(what)
+            if what[0] == "gram":
+                now += 0.3
+                if what[1] < 5:
+                    gram_sends(now, what[1])
+                    launch(held.get(what[1], []))
+                else:
+                    now += 1.0
+                    chol = [c for b in range(6) for c in [("chol", b, p) for p in range(4)] + [("block", b)]]
+            else:
+                _, name, s = what
+                _, axis, way, size, _ = specs[name]
+                now += 0.1 + size / 3e6
+                if s < SIZES[axis] - 2:
+                    post(wire(now, axis, way, size), ("serve", name, s + 1))
+                else:
+                    ended.add(name)
+                    for other, spec in specs.items():
+                        if name in spec[4] and all(x in ended for x in spec[4]):
+                            begin(now, other)
+                            plan.append(("begin", [other]))
+        else:
+            what = chol.pop(0)
+            plan.append(what)
+            now += 1.35 if what[0] == "chol" else 2.0
+            chol_end = now
+    return plan, now, chol_end
 
 
 class Stream:
@@ -321,9 +427,6 @@
     return pl.multiple_of(i * 140 // 8 * 8, 8)
 
 
-Z_ROWS = ((1, 0, 144), (1, 144, 136), (-1, 280, 144), (-1, 424, 136))
-Y_ROWS = ((1, 0, 40), (1, 40, 32), (-1, 72, 40), (-1, 112, 32))
-ZY_ROWS = ((1, 0, 72), (-1, 72, 72))
 RS_COPIES = 4 * 7 + 4 * 3 + 2 * 3 + 4 * 7
 
 
@@ -348,111 +451,89 @@
             c[q // 35, pl.ds(pl.multiple_of(lax.rem(q, 35) * 16, 16), 16), :] = value[k * 16:(k + 1) * 16, :]
         return 0
 
-    lax.fori_loop(0, 20, tile, 0)
-    next(exchange)
-    lax.fori_loop(20, tiles, tile, 0)
-    next(exchange)
-
-    base = 0
-    zs, ys, zys, yzs = [], [], [], []
-    for k, (way, o, n) in enumerate(Z_ROWS):
-        local = lambda i, o=o, n=n: c.at[i, o:o + n, 0:HALF]
-        zs.append(Stream("z", way, local, zb[k], resz.at[o:o + n], sems, base))
-        base += NZ - 1
-    for k, (way, o, n) in enumerate(Y_ROWS):
-        local = lambda i, o=o, n=n: c.at[:, pl.ds(sub_start(i) + o, n), HALF:2 * HALF]
-        ys.append(Stream("y", way, local, yb[k], resy.at[:, o:o + n], sems, base))
-        base += NY - 1
-    for k, (way, o, n) in enumerate(ZY_ROWS):
-        local = lambda i, o=o, n=n: resz.at[pl.ds(sub_start(i) + o, n)]
-        zys.append(Stream("y", way, local, zyb[k], out.at[o:o + n, 0:HALF], sems, base))
-        base += NY - 1
-    for k, (way, o, n) in enumerate(Y_ROWS):
-        local = lambda i, o=o, n=n: resy.at[i, o:o + n]
-        yzs.append(Stream("z", way, local, yzb[k], out.at[o:o + n, HALF:2 * HALF], sems, base))
-        base += NZ - 1
-    for k in (0, 2, 1, 3):
-        zs[k].copy(0).start()
-        ys[k].copy(0).start()
-
-    events = []
-    def later(when, action):
-        events.append((when, len(events), action))
-    for step in range(NZ - 1):
-        for k in (0, 2, 1, 3):
-            later(9.3 * (step + 1) + (1.7 if k % 2 else -2.9), lambda k=k, step=step: zs[k].serve(step))
-    for step in range(NY - 1):
-        for k in (0, 2, 1, 3):
-            later(19 * (step + 1) + (1.7 if k % 2 else -6.8), lambda k=k, step=step: ys[k].serve(step))
-    later(67, lambda: [x.copy(0).start() for x in zys])
-    later(58.8, lambda: [yzs[k].copy(0).start() for k in (0, 2, 1, 3)])
-    for step in range(NY - 1):
-        for k in (0, 1):
-            later(71 + 4 * step, lambda k=k, step=step: zys[k].serve(step))
-    for step in range(NZ - 1):
-        for k in (0, 2, 1, 3):
-            later(62.5 + 3.3 * step, lambda k=k, step=step: yzs[k].serve(step))
-    events.sort(key=lambda e: e[:2])
-
-    def due(now):
-        ready = []
-        while events and events[0][0] <= now:
-            ready.append(events.pop(0)[2])
-        return ready
-
-    next(exchange)
-    now = 8
-    for cost in (10, 4):
-        for action in due(now):
-            action()
-        now += cost
-        try:
-            next(exchange)
-        except StopIteration:
-            pass
-    for action in due(now):
-        action()
-    for _ in exchange:
-        pass
+    start = lax.rem(lax.axis_index("z") + NZ - 1, NZ) * (slab.shape[1] // NZ) // B
+    early = 15
+
+    def tiles_of(lo, hi):
+        lax.fori_loop(lo, hi, lambda t, _: tile(lax.rem(start + t, tiles), 0), 0)
+
+    streams, base = {}, 0
+    for kind, axis, rows in KINDS:
+        for k, (way, o, n) in enumerate(rows):
+            buf, sink = {
+                "z": lambda: (zb[k], resz.at[o:o + n]),
+                "y": lambda: (yb[k], resy.at[:, o:o + n]),
+                "zy": lambda: (zyb[k], out.at[o:o + n, 0:HALF]),
+                "yz": lambda: (yzb[k], out.at[o:o + n, HALF:2 * HALF]),
+            }[kind]()
+            local = functools.partial(lambda i, kind, o, n: {
+                "z": lambda: c.at[i, o:o + n, 0:HALF],
+                "y": lambda: c.at[:, pl.ds(sub_start(i) + o, n), HALF:2 * HALF],
+                "zy": lambda: resz.at[pl.ds(sub_start(i) + o, n)],
+                "yz": lambda: resy.at[i, o:o + n],
+            }[kind](), kind=kind, o=o, n=n)
+            streams[kind, k] = Stream(axis, way, local, buf, sink, sems, base)
+            base += SIZES[axis] - 1
+
     n = 6
-    for i in range(n):
-        for j in range(i + 1):
-            t = i * (i + 1) // 2 + j
-            a[i * B:(i + 1) * B, j * B:(j + 1) * B] = full[t // 6, t // 3 % 2, (t % 3) * B:(t % 3 + 1) * B, :]
+
+    def act(what):
+        if what[0] == "gram":
+            next(exchange, None)
+            if what[1] == 5:
+                for i in range(n):
+                    for j in range(i + 1):
+                        t = i * (i + 1) // 2 + j
+                        a[i * B:(i + 1) * B, j * B:(j + 1) * B] = full[t // 6, t // 3 % 2, (t % 3) * B:(t % 3 + 1) * B, :]
+        elif what[0] == "begin":
+            for name in what[1]:
+                streams[name].copy(0).start()
+        elif what[0] == "serve":
+            streams[what[1]].serve(what[2])
+        elif what[0] == "tiles":
+            tiles_of(early, tiles)
+
+    plan = finish_plan()[0]
+    first = next(i for i, what in enumerate(plan) if what[0] == "chol")
+    last = max(i for i, what in enumerate(plan) if what[0] == "block")
+    table, key = {}, None
+    for what in plan[first:last + 1]:
+        if what[0] == "chol":
+            key = what[1], what[2]
+        elif what[0] == "block":
+            key = what[1], 4
+        else:
+            table.setdefault(key, []).append(what)
+
+    tiles_of(0, early)
     w[...] = jnp.zeros_like(w)
+    for what in plan[:first]:
+        act(what)
     row_of = lax.broadcasted_iota(jnp.int32, (B, B), 0)
     col_of = lax.broadcasted_iota(jnp.int32, (B, B), 1)
     eye = jnp.where(row_of == col_of, 1.0, 0.0).astype(F32)
-    table = {}
-    for b in range(n):
-        for piece in range(4):
-            now += 1.35
-            table[b, piece] = due(now)
-            now += 0.3 * len(table[b, piece])
-        now += 2
 
     def step(b, _):
         o = pl.multiple_of(b * B, B)
         m[:, :B] = a[pl.ds(o, B), pl.ds(o, B)]
         m[:, B:] = eye
-        for piece in range(4):
-            factor_panels(m, v, 4 * piece, 4 * piece + 4)
+        for piece in range(5):
+            if piece < 4:
+                factor_panels(m, v, 4 * piece, 4 * piece + 4)
             for k in range(n):
-                if table[k, piece]:
+                if piece == 4 or table.get((k, piece)):
                     @pl.when(b == k)
                     def _():
-                        for action in table[k, piece]:
-                            action()
-        for k in range(n):
-            @pl.when(b == k)
-            def _():
-                chol_block(a, w, lfac, m, v, k)
+                        if piece == 4:
+                            chol_block(a, w, lfac, m, v, k)
+                        for what in table.get((k, piece), ()):
+                            act(what)
         return 0
 
     lax.fori_loop(0, n, step, 0)
-    for action in due(1e9):
-        action()
-    for stream in (*zs, *ys, *zys, *yzs):
+    for what in plan[last + 1:]:
+        act(what)
+    for stream in streams.values():
         stream.finish()
 
 

time: 241 us -> 218 us (0.905)
  Pallas kernels: 205 us -> 183 us
    pallas_call x1, Pallas kernels: 64.8 us -> 50.5 us  [gather(): pl.pallas_call(functools.partial(gather_kernel, plan), out_shape=jax.Shap...]
    pallas_call x1, Pallas kernels: 119 us -> 112 us  [finish(): pl.pallas_call(finish_kernel, out_shape=(jax.ShapeDtypeStruct((144, C), F...]
where the time goes in v2:
time: 218 us
  Pallas kernels  183 us (84%)
  blocking collectives  24.4 us (11%)
  matrix products  9.59 us (4%)
    pallas_call x1, Pallas kernels, finish(): pl.pallas_call(finish_kernel, out_shape=(jax.ShapeDtypeStruct((144, C), F...  112 us
    pallas_call x1, Pallas kernels, gather(): pl.pallas_call(functools.partial(gather_kernel, plan), out_shape=jax.Shap...  50.5 us
    all_to_all x1, blocking collectives, body(): p = lax.all_to_all(p.reshape(NZ * NY, 24, -1), ('z', 'y'), 0, 0, tiled=True)  24.4 us
    pallas_call x1, Pallas kernels, total_over_aux(): pl.pallas_call(total_kernel, out_shape=jax.ShapeDtypeStruct((R, C), F32),...  20.5 us
    dot_general x1, matrix products, body(): lax.dot_general(slab, tests, (NT, ((), ())), preferred_element_type=F32)  5.86 us

profile of v2, /device:TPU:8, one launch (start us, length us, event | category | flops | bytes accessed | tf_op | source)
XLA Modules:
  0.0 218.0 jit_solution(2182582622320529790)
XLA Ops:
  0.0 0.0 copy-start
  0.0 50.5 %gather.1 = bf16[8,4,24,4480]{3,2,1,0:T(8,128)(2,1)} custom-call(bf16[24,4480]{1,0:T(8,128)(2,1)} %bitcast.10), custom_call_target="tpu_custom_call" | custom-call | tf_op jit(solution)/shard_map/gather/pallas_call | solution.py:183
  50.5 0.0 copy-done
  50.5 5.9 %fusion.3.part = f32[256,768]{1,0:T(8,128)} fusion(bf16[256,4480]{1,0:T(8,128)(2,1)S(1)} %copy-done, bf16[768,4480]{1,0:T(8,128)(2,1)} %bitcast.7), kind=kOutput, calls=%fused_computation.3 | convolution fusion | flops 1761607680 | bytes 9961472 | tf_op jit(solution)/shard_map/dot_general | solution.py:564
  56.4 20.5 %total.1.s = f32[256,768]{1,0:T(8,128)} custom-call(f32[256,768]{1,0:T(8,128)} %fusion.3.part), custom_call_target="tpu_custom_call" | custom-call | tf_op jit(solution)/shard_map/total/pallas_call | solution.py:226
  76.8 111.6 %finish.1 = (f32[144,768]{1,0:T(8,128)}, f32[768,768]{1,0:T(8,128)}) custom-call(bf16[256,4480]{1,0:T(8,128)(2,1)} %slab.1, f32[256,768]{1,0:T(8,128)} %total.1.s), custom_call_target="tpu_custom_call" | custom-call | tf_op jit(solution)/shard_map/finish/pallas_call | solution.py:544
  188.4 3.7 %fusion = f32[768,140]{1,0:T(8,128)S(1)} fusion(f32[768,768]{1,0:T(8,128)} %get-tuple-element.7, f32[144,768]{1,0:T(8,128)} %get-tuple-element.8, s32[]{:T(128)S(6)} %select_n.11), kind=kOutput, calls=%fused_computation | convolution fusion | flops 990904320 | bytes 3231748 | tf_op jit(solution)/shard_map/dot_general | solution.py:569
  192.2 24.4 %all_to_all.5 = f32[32,24,140]{2,1,0:T(8,128)S(1)} all-to-all(f32[32,24,140]{2,1,0:T(8,128)S(1)} %bitcast.9), channel_id=1, replica_groups=mesh['z'=8,'y'=4,'x'=4,'c'=2] {'z','y'}, dimensions={0} | all-to-all | bytes 860160 | tf_op jit(solution)/shard_map/all_to_all | solution.py:570
  216.6 0.3 copy.6
  216.8 1.1 reshape.11
Async XLA Ops:
  0.0 50.5 %copy-start = (bf16[256,4480]{1,0:T(8,128)(2,1)S(1)}, bf16[256,4480]{1,0:T(8,128)(2,1)}, u32[]{:S(2)}) copy-start(bf16[256,4480]{1,0:T(8,128)(2,1)} %slab.1) | copy-start | bytes 6881284

commit v3 on v2

--- a/solution.py
+++ b/solution.py
@@ -112,123 +112,176 @@
 RATE, HOP = 42e3, 2.0
 
 
-def gather_plan(d, cut, K):
-    free, heap, plan, count = {}, [], [], 0
+def sketch_plan(d, cut, K):
+    free, heap, plan, count, order = {}, [], [], 0, 0
+    missing = {dz: NY * K for dz in range(NZ)}
+
+    def post(when, what):
+        nonlocal order
+        order += 1
+        heapq.heappush(heap, (when, order, what))
 
     def start(now, phase, way, step, dz, dy, lo, hi):
         nonlocal count
         axis = phase[1]
-        begin = max(now, free.get((axis, way), 0.0))
-        end = begin + d * (hi - lo) * 2 / RATE
+        end = max(now, free.get((axis, way), 0.0)) + d * (hi - lo) * 2 / RATE
         free[axis, way] = end
         job = (phase, axis, way, step, dz, dy, lo, hi, count)
         count += 1
-        heapq.heappush(heap, (end + HOP, count, job))
+        post(end + HOP, ("got", job))
         return job
 
     def both(now, phase, dz, dy, lo, hi):
         return [start(now, phase, way, 0, dz, dy, lo, hi) for way in (1, -1)]
 
+    def share(now, axis, size, lag):
+        end = max(now, free.get(axis, 0.0)) + size / (100e3 if axis == "c" else RATE / 2)
+        free[axis] = end
+        return end + lag
+
     first = both(0, "ly", 0, 0, 0, cut) + both(0, "rz", 0, 0, cut, K)
     first += both(0, "lz", 0, 0, 0, cut) + both(0, "ry", 0, 0, cut, K)
-    plan.append((None, first))
+    plan.append(("got", None, first))
+    missing[0] -= K
     now = 0.0
+    rows = NY * d
     while heap:
-        when, _, job = heapq.heappop(heap)
+        when, _, what = heapq.heappop(heap)
         now = max(now, when) + 0.05
-        phase, axis, way, step, dz, dy, lo, hi, _ = job
-        dz, dy = (dz - way, dy) if axis == "z" else (dz, dy - way)
-        mid = lo + ((hi - lo) // 128 + 1) // 2 * 128
-        far = SIZES[axis] // 2
-        new = []
-        if step < far - 1:
-            a, b = (lo, hi) if step < far - 2 else ((lo, mid) if way == 1 else (mid, hi))
-            if b > a:
-                new.append(start(now, phase, way, step + 1, dz, dy, a, b))
-        if phase in ("ly", "rz"):
-            new += both(now, "lz" if phase == "ly" else "ry", dz, dy, lo, hi)
-        plan.append((job, new))
+        if what[0] == "got":
+            job = what[1]
+            phase, axis, way, step, dz, dy, lo, hi, _ = job
+            dz, dy = (dz - way, dy) if axis == "z" else (dz, dy - way)
+            mid = lo + ((hi - lo) // 128 + 1) // 2 * 128
+            far = SIZES[axis] // 2
+            new = []
+            if step < far - 1:
+                a, b = (lo, hi) if step < far - 2 else ((lo, mid) if way == 1 else (mid, hi))
+                if b > a:
+                    new.append(start(now, phase, way, step + 1, dz, dy, a, b))
+            if phase in ("ly", "rz"):
+                new += both(now, "lz" if phase == "ly" else "ry", dz, dy, lo, hi)
+            plan.append(("got", job, new))
+            missing[dz % NZ] -= hi - lo
+            if not missing[dz % NZ]:
+                post(now + 0.3, ("product", dz % NZ))
+        elif what[0] == "product":
+            plan.append(what)
+            now += 1.5
+            post(share(now, "c", rows * 512, 1.5), ("sum", what[1], 1))
+        else:
+            _, dz, stage = what
+            plan.append(what)
+            now += 0.2
+            if stage < 3:
+                post(share(now, "x", rows * 128 * 3, HOP + 1), ("sum", dz, stage + 1))
+            elif stage == 3:
+                post(share(now, "c", rows * 512, 1.5), ("sum", dz, 4))
     return plan, count, now
 
 
-def gather_kernel(plan, t, g, send_sems, recv_sems, own_sem):
-    z, y = lax.axis_index("z"), lax.axis_index("y")
+def sketch_kernel(plan, t, slab, st, g, part, near, acc, far, gs, gr, ss, sr, own_sem):
+    z, y, x, c = (lax.axis_index(axis) for axis in AXES)
+    d = t.shape[0] * 8
+    rows, piece = NY * d, NY * d // NX
+    half = st.shape[1] // 2
+
+    def place(dz, dy, lo, hi):
+        at = (lax.rem(z + dz + NZ, NZ) * NY + lax.rem(y + dy + NY, NY)) * d
+        return g.at[pl.ds(at // 8, d // 8), :, lo:hi]
 
     def copy(job):
         phase, axis, way, step, dz, dy, lo, hi, k = job
-        place = g.at[lax.rem(z + dz + NZ, NZ), lax.rem(y + dy + NY, NY), :, lo:hi]
+        to = place(dz, dy, lo, hi)
         return pltpu.make_async_remote_copy(
-            src_ref=t.at[:, lo:hi] if dz == dy == 0 else place, dst_ref=place,
-            send_sem=send_sems.at[k], recv_sem=recv_sems.at[k],
+            src_ref=t.at[:, :, lo:hi] if dz == dy == 0 else to, dst_ref=to, send_sem=gs.at[k], recv_sem=gr.at[k],
             device_id={axis: step_to(axis, 1 if way == 1 else SIZES[axis] - 1)}, device_id_type=MESH,
         )
 
-    greet([("y", 1), ("y", NY - 1), ("z", 1), ("z", NZ - 1)])
-    for job, new in plan:
-        if job is not None:
-            copy(job).wait_recv()
-        for other in new:
-            copy(other).start()
-        if job is None:
-            keep = pltpu.make_async_copy(t, g.at[z, y], own_sem)
-            keep.start()
-    keep.wait()
-    for job, _ in plan[1:]:
-        copy(job).wait_send()
-
-
-def gather(t):
+    def rows_of(dz):
+        return pl.multiple_of(lax.rem(z + dz, NZ) * rows, 8)
+
+    def lanes_of(core):
+        return pl.ds(pl.multiple_of(core * half, half), half)
+
+    def remote(src, dst, k, axis, hops):
+        return pltpu.make_async_remote_copy(
+            src_ref=src, dst_ref=dst, send_sem=ss.at[k], recv_sem=sr.at[k],
+            device_id={axis: step_to(axis, hops)}, device_id_type=MESH,
+        )
+
+    def exchange(dz, stage):
+        k = dz * 8
+        if stage == 1:
+            return [remote(part.at[dz, :, lanes_of(1 - c)], near.at[dz], k, "c", 1)]
+        if stage == 2:
+            return [remote(acc.at[dz, pl.ds(pl.multiple_of(step_to("x", i) * piece, 8), piece)], far.at[dz, i - 1], k + i, "x", i) for i in (1, 2, 3)]
+        if stage == 3:
+            own = st.at[pl.ds(pl.multiple_of(rows_of(dz) + x * piece, 8), piece), lanes_of(c)]
+            return [remote(own, own, k + 3 + i, "x", i) for i in (1, 2, 3)]
+        all_mine = st.at[pl.ds(rows_of(dz), rows), lanes_of(c)]
+        return [remote(all_mine, all_mine, k + 7, "c", 1)]
+
+    def begin(dz, stage):
+        for one in exchange(dz, stage):
+            one.start()
+
+    greet([("y", 1), ("y", NY - 1), ("z", 1), ("z", NZ - 1), ("c", 1)] + [("x", i) for i in (1, 2, 3)])
+    keep = pltpu.make_async_copy(t, place(0, 0, 0, t.shape[2]), own_sem)
+    kept = False
+    for what in plan:
+        if what[0] == "got":
+            if what[1] is not None:
+                copy(what[1]).wait_recv()
+            for job in what[2]:
+                copy(job).start()
+            if what[1] is None:
+                keep.start()
+        elif what[0] == "product":
+            dz = what[1]
+            if not kept:
+                keep.wait()
+                kept = True
+            part[dz] = lax.dot_general(g[pl.ds(rows_of(dz) // 8, rows // 8)].reshape(rows, g.shape[2]), slab[...], (NT, ((), ())), preferred_element_type=F32)
+            begin(dz, 1)
+        else:
+            _, dz, stage = what
+            for one in exchange(dz, stage):
+                one.wait_recv()
+            if stage == 1:
+                acc[dz] = part[dz, :, lanes_of(c)] + near[dz]
+            elif stage == 2:
+                mine = pl.multiple_of(x * piece, 8)
+                total = acc[dz, pl.ds(mine, piece), :]
+                for i in range(3):
+                    total = total + far[dz, i]
+                st[pl.ds(pl.multiple_of(rows_of(dz) + mine, 8), piece), lanes_of(c)] = total
+            if stage < 4:
+                begin(dz, stage + 1)
+    for what in plan:
+        if what[0] == "got" and what[1] is not None:
+            copy(what[1]).wait_send()
+        elif what[0] == "sum":
+            for one in exchange(what[1], what[2]):
+                one.wait_send()
+
+
+def sketch_of(t, slab):
     d, K = t.shape
-    plan, count, _ = gather_plan(d, K // 128 * 2 // 5 * 128, K)
-    g = pl.pallas_call(
-        functools.partial(gather_kernel, plan), out_shape=jax.ShapeDtypeStruct((NZ, NY, d, K), t.dtype),
-        in_specs=[ANY], out_specs=ANY,
-        scratch_shapes=[DMA((count,)), DMA((count,)), DMA],
-        compiler_params=pltpu.CompilerParams(collective_id=0, has_side_effects=True), name="gather",
-    )(t)
-    return g.reshape(NZ * NY * d, K)
-
-
-def total_kernel(part, out, near, acc, far, send_sems, recv_sems):
-    x, c = lax.axis_index("x"), lax.axis_index("c")
-    R = part.shape[0]
-    h, q = R // 2, R // 8
-    sems = (send_sems, recv_sems)
-    greet([("c", 1)] + [("x", i) for i in (1, 2, 3)])
-    mine = pl.multiple_of(c * h, h)
-    other = pl.multiple_of((1 - c) * h, h)
-    first = send(part.at[pl.ds(other, h)], near, sems, 0, "c", 1)
-    first.wait_recv()
-    acc[...] = part[pl.ds(mine, h), :] + near[...]
-    spread = []
-    for i in (1, 2, 3):
-        o = pl.multiple_of(step_to("x", i) * q, q)
-        spread.append(send(acc.at[pl.ds(o, q)], far.at[i - 1], sems, i, "x", i))
-    o = pl.multiple_of(x * q, q)
-    total = acc[pl.ds(o, q), :]
-    for i in (1, 2, 3):
-        spread[i - 1].wait_recv()
-        total = total + far[i - 1]
-    own = pl.ds(pl.multiple_of(mine + o, q), q)
-    out[own, :] = total
-    back = [send(out.at[own], out.at[own], sems, 3 + i, "x", i) for i in (1, 2, 3)]
-    for b in back:
-        b.wait_recv()
-    half = out.at[pl.ds(mine, h)]
-    last = send(half, half, sems, 7, "c", 1)
-    last.wait_recv()
-    for copy in (first, *spread, *back, last):
-        copy.wait_send()
-
-
-def total_over_aux(part):
-    R, C = part.shape
+    R = slab.shape[0]
+    plan, count, _ = sketch_plan(d, K // 128 * 2 // 5 * 128, K)
+    n, rows = NZ * NY * d, NY * d
     return pl.pallas_call(
-        total_kernel, out_shape=jax.ShapeDtypeStruct((R, C), F32),
-        in_specs=[VM], out_specs=VM,
-        scratch_shapes=[pltpu.VMEM((R // 2, C), F32), pltpu.VMEM((R // 2, C), F32), pltpu.VMEM((3, R // 8, C), F32), DMA((8,)), DMA((8,))],
-        compiler_params=pltpu.CompilerParams(collective_id=1, has_side_effects=True), name="total",
-    )(part)
+        functools.partial(sketch_kernel, plan),
+        out_shape=jax.ShapeDtypeStruct((n, R), F32),
+        in_specs=[ANY, VM], out_specs=VM,
+        scratch_shapes=[
+            pltpu.VMEM((n // 8, 8, K), t.dtype),
+            pltpu.VMEM((NZ, rows, R), F32), pltpu.VMEM((NZ, rows, R // 2), F32), pltpu.VMEM((NZ, rows, R // 2), F32),
+            pltpu.VMEM((NZ, 3, rows // NX, R // 2), F32), DMA((count,)), DMA((count,)), DMA((64,)), DMA((64,)), DMA,
+        ],
+        compiler_params=pltpu.CompilerParams(collective_id=0, has_side_effects=True, vmem_limit_bytes=40 * 2**20), name="sketch",
+    )(t.reshape(d // 8, 8, K), slab)
 
 
 SLOTS = 3
@@ -246,9 +299,9 @@
     a = lax.axis_index("x") * 2 + lax.axis_index("c")
     for k in range(SLOTS):
         i, j = place(a * SLOTS + k)
-        li = s[:, pl.ds(pl.multiple_of(i * B, B), B)]
-        lj = s[:, pl.ds(pl.multiple_of(j * B, B), B)]
-        gp[k * B:(k + 1) * B, :] = dot(li, lj, TN)
+        li = s[pl.ds(pl.multiple_of(i * B, B), B), :]
+        lj = s[pl.ds(pl.multiple_of(j * B, B), B), :]
+        gp[k * B:(k + 1) * B, :] = dot(li, lj, NT)
 
 
 GRAM_PEERS = [("z", i) for i in range(1, NZ)] + [("y", i) for i in range(1, NY)] + [("x", i) for i in range(1, NX)] + [("c", 1)]
@@ -439,8 +492,11 @@
     exchange = gram_exchange(gp, gz, own, gy, full, (gs, gr), 0)
     gram_compute(s, gp)
     next(exchange)
-    hi[...] = s[...].astype(jnp.bfloat16)
-    lo[...] = (s[...] - hi[...].astype(F32)).astype(jnp.bfloat16)
+    for k in range(s.shape[0] // B):
+        turned = s[k * B:(k + 1) * B, :].T
+        top = turned.astype(jnp.bfloat16)
+        hi[:, k * B:(k + 1) * B] = top
+        lo[:, k * B:(k + 1) * B] = (turned - top.astype(F32)).astype(jnp.bfloat16)
 
     def tile(t, _):
         part = slab[:, pl.ds(pl.multiple_of(t * B, B), B)]
@@ -539,7 +595,7 @@
 
 def finish(slab, s):
     bf = jnp.bfloat16
-    R, C = s.shape
+    C, R = s.shape
     vm = lambda *shape: pltpu.VMEM(shape, F32)
     return pl.pallas_call(
         finish_kernel,
@@ -560,10 +616,7 @@
 
 
 def body(slab, test):
-    tests = gather(test.T)
-    part = lax.dot_general(slab, tests, (NT, ((), ())), preferred_element_type=F32)
-    sketch = total_over_aux(part)
-    c, w = finish(slab, sketch)
+    c, w = finish(slab, sketch_of(test.T, slab))
     y = lax.axis_index("y")
     c = lax.dynamic_slice_in_dim(c, y * 140 % 8, 140, 0)
     p = lax.dot_general(w, c, (NT, ((), ())), precision=HI, preferred_element_type=F32)

time: 218 us -> 207 us (0.950)
  Pallas kernels: 183 us -> 174 us
  matrix products: 9.59 us -> 3.74 us
  local copies, waits for them, and re-layouts: 1.4 us -> 4.86 us
    pallas_call x2 -> x1, Pallas kernels: 70.9 us -> 63.2 us  [sketch_of(): pl.pallas_call(functools.partial(sketch_kernel, plan), out_shape=jax.Shap...]
    dot_general x1 -> x0, matrix products: 5.86 us -> none  [body(): lax.dot_general(slab, tests, (NT, ((), ())), preferred_element_type=F32)]
    unnamed x2 -> x6, local copies, waits for them, and re-layouts: 0.01 us -> 3.46 us
where the time goes in v3:
time: 207 us
  Pallas kernels  174 us (84%)
  blocking collectives  24.7 us (12%)
  local copies, waits for them, and re-layouts  4.86 us (2%)
  matrix products  3.74 us (2%)
    pallas_call x1, Pallas kernels, finish(): pl.pallas_call(finish_kernel, out_shape=(jax.ShapeDtypeStruct((144, C), F...  110 us
    pallas_call x1, Pallas kernels, sketch_of(): pl.pallas_call(functools.partial(sketch_kernel, plan), out_shape=jax.Shap...  63.2 us
    all_to_all x1, blocking collectives, body(): p = lax.all_to_all(p.reshape(NZ * NY, 24, -1), ('z', 'y'), 0, 0, tiled=True)  24.7 us

profile of v3, /device:TPU:8, one launch (start us, length us, event | category | flops | bytes accessed | tf_op | source)
XLA Modules:
  0.0 207.0 jit_solution(17428016445000132678)
XLA Ops:
  0.0 0.0 copy-start
  0.0 1.6 copy-done
  1.6 0.0 copy-start.2
  1.6 0.9 copy-done.2
  2.6 63.2 %sketch.1.s = f32[768,256]{1,0:T(8,128)S(1)} custom-call(bf16[3,8,4480]{2,1,0:T(8,128)(2,1)S(1)} %bitcast.6, bf16[256,4480]{1,0:T(8,128)(2,1)S(1)} %copy-done), custom_call_target="tpu_custom_call" | custom-call | tf_op jit(solution)/shard_map/sketch/pallas_call | solution.py:274
  65.8 0.0 copy-start.1
  65.8 0.9 copy-done.1
  66.7 110.5 %finish.1 = (f32[144,768]{1,0:T(8,128)}, f32[768,768]{1,0:T(8,128)}) custom-call(bf16[256,4480]{1,0:T(8,128)(2,1)} %slab.3, f32[768,256]{1,0:T(8,128)} %copy-done.1), custom_call_target="tpu_custom_call" | custom-call | tf_op jit(solution)/shard_map/finish/pallas_call | solution.py:600
  177.2 3.7 %fusion = f32[768,140]{1,0:T(8,128)S(1)} fusion(f32[768,768]{1,0:T(8,128)} %get-tuple-element.7, f32[144,768]{1,0:T(8,128)} %get-tuple-element.8, s32[]{:T(128)S(6)} %select_n.11), kind=kOutput, calls=%fused_computation | convolution fusion | flops 990904320 | bytes 3231748 | tf_op jit(solution)/shard_map/dot_general | solution.py:622
  180.9 24.7 %all_to_all.5 = f32[32,24,140]{2,1,0:T(8,128)S(1)} all-to-all(f32[32,24,140]{2,1,0:T(8,128)S(1)} %bitcast.8), channel_id=1, replica_groups=mesh['z'=8,'y'=4,'x'=4,'c'=2] {'z','y'}, dimensions={0} | all-to-all | bytes 860160 | tf_op jit(solution)/shard_map/all_to_all | solution.py:623
  205.6 0.3 copy.6
  205.8 1.1 reshape.11
Async XLA Ops:
  0.0 1.6 copy-start
  1.6 0.9 copy-start.2
  65.8 0.9 copy-start.1

commit v4 on v3

--- a/solution.py
+++ b/solution.py
@@ -173,17 +173,17 @@
             _, dz, stage = what
             plan.append(what)
             now += 0.2
-            if stage < 3:
-                post(share(now, "x", rows * 128 * 3, HOP + 1), ("sum", dz, stage + 1))
-            elif stage == 3:
-                post(share(now, "c", rows * 512, 1.5), ("sum", dz, 4))
+            if stage == 1:
+                post(share(now, "x", rows * 512, HOP + 1), ("sum", dz, 2))
+            elif stage == 2:
+                post(share(now, "c", rows * 512, 1.5), ("sum", dz, 3))
     return plan, count, now
 
 
-def sketch_kernel(plan, t, slab, st, g, part, near, acc, far, gs, gr, ss, sr, own_sem):
+def sketch_part(plan, t, slab, slab_copy, st, g, part, near, acc, far, gs, gr, ss, sr, own_sem):
     z, y, x, c = (lax.axis_index(axis) for axis in AXES)
     d = t.shape[0] * 8
-    rows, piece = NY * d, NY * d // NX
+    rows = NY * d
     half = st.shape[1] // 2
 
     def place(dz, dy, lo, hi):
@@ -211,22 +211,18 @@
         )
 
     def exchange(dz, stage):
-        k = dz * 8
+        k = dz * 5
         if stage == 1:
             return [remote(part.at[dz, :, lanes_of(1 - c)], near.at[dz], k, "c", 1)]
         if stage == 2:
-            return [remote(acc.at[dz, pl.ds(pl.multiple_of(step_to("x", i) * piece, 8), piece)], far.at[dz, i - 1], k + i, "x", i) for i in (1, 2, 3)]
-        if stage == 3:
-            own = st.at[pl.ds(pl.multiple_of(rows_of(dz) + x * piece, 8), piece), lanes_of(c)]
-            return [remote(own, own, k + 3 + i, "x", i) for i in (1, 2, 3)]
+            return [remote(acc.at[dz], far.at[dz, x], k + i, "x", i) for i in (1, 2, 3)]
         all_mine = st.at[pl.ds(rows_of(dz), rows), lanes_of(c)]
-        return [remote(all_mine, all_mine, k + 7, "c", 1)]
+        return [remote(all_mine, all_mine, k + 4, "c", 1)]
 
     def begin(dz, stage):
         for one in exchange(dz, stage):
             one.start()
 
-    greet([("y", 1), ("y", NY - 1), ("z", 1), ("z", NZ - 1), ("c", 1)] + [("x", i) for i in (1, 2, 3)])
     keep = pltpu.make_async_copy(t, place(0, 0, 0, t.shape[2]), own_sem)
     kept = False
     for what in plan:
@@ -241,6 +237,7 @@
             dz = what[1]
             if not kept:
                 keep.wait()
+                slab_copy.wait()
                 kept = True
             part[dz] = lax.dot_general(g[pl.ds(rows_of(dz) // 8, rows // 8)].reshape(rows, g.shape[2]), slab[...], (NT, ((), ())), preferred_element_type=F32)
             begin(dz, 1)
@@ -249,14 +246,15 @@
             for one in exchange(dz, stage):
                 one.wait_recv()
             if stage == 1:
-                acc[dz] = part[dz, :, lanes_of(c)] + near[dz]
+                total = part[dz, :, lanes_of(c)] + near[dz]
+                acc[dz] = total
+                far[dz, x] = total
             elif stage == 2:
-                mine = pl.multiple_of(x * piece, 8)
-                total = acc[dz, pl.ds(mine, piece), :]
-                for i in range(3):
-                    total = total + far[dz, i]
-                st[pl.ds(pl.multiple_of(rows_of(dz) + mine, 8), piece), lanes_of(c)] = total
-            if stage < 4:
+                total = far[dz, 0]
+                for other in range(1, NX):
+                    total = total + far[dz, other]
+                st[pl.ds(rows_of(dz), rows), lanes_of(c)] = total
+            if stage < 3:
                 begin(dz, stage + 1)
     for what in plan:
         if what[0] == "got" and what[1] is not None:
@@ -264,24 +262,6 @@
         elif what[0] == "sum":
             for one in exchange(what[1], what[2]):
                 one.wait_send()
-
-
-def sketch_of(t, slab):
-    d, K = t.shape
-    R = slab.shape[0]
-    plan, count, _ = sketch_plan(d, K // 128 * 2 // 5 * 128, K)
-    n, rows = NZ * NY * d, NY * d
-    return pl.pallas_call(
-        functools.partial(sketch_kernel, plan),
-        out_shape=jax.ShapeDtypeStruct((n, R), F32),
-        in_specs=[ANY, VM], out_specs=VM,
-        scratch_shapes=[
-            pltpu.VMEM((n // 8, 8, K), t.dtype),
-            pltpu.VMEM((NZ, rows, R), F32), pltpu.VMEM((NZ, rows, R // 2), F32), pltpu.VMEM((NZ, rows, R // 2), F32),
-            pltpu.VMEM((NZ, 3, rows // NX, R // 2), F32), DMA((count,)), DMA((count,)), DMA((64,)), DMA((64,)), DMA,
-        ],
-        compiler_params=pltpu.CompilerParams(collective_id=0, has_side_effects=True, vmem_limit_bytes=40 * 2**20), name="sketch",
-    )(t.reshape(d // 8, 8, K), slab)
 
 
 SLOTS = 3
@@ -483,12 +463,18 @@
 RS_COPIES = 4 * 7 + 4 * 3 + 2 * 3 + 4 * 7
 
 
-def finish_kernel(slab, s, out, w, c, resz, resy, *rest):
+def whole_kernel(plan, t, slab_in, p, slab, slab_sem, st, g, part, near, acc, far, ts, tr, us, ur, own_sem, *rest):
+    out, w, c, resz, resy = rest[:5]
+    rest = rest[5:]
     zb, yb, zyb, yzb = rest[0:4], rest[4:8], rest[8:10], rest[10:14]
     hi, lo, gp, gz, own, gy, full, a, lfac, m, v, ss, rs, gs, gr = rest[14:]
+    slab_copy = pltpu.make_async_copy(slab_in, slab, slab_sem)
+    slab_copy.start()
+    greet(GRAM_PEERS)
+    sketch_part(plan, t, slab, slab_copy, st, g, part, near, acc, far, ts, tr, us, ur, own_sem)
+    s = st
     sems = (ss, rs)
     tiles = slab.shape[1] // B
-    greet(GRAM_PEERS)
     exchange = gram_exchange(gp, gz, own, gy, full, (gs, gr), 0)
     gram_compute(s, gp)
     next(exchange)
@@ -589,19 +575,34 @@
     lax.fori_loop(0, n, step, 0)
     for what in plan[last + 1:]:
         act(what)
+    odd = lax.rem(lax.axis_index("y"), 2)
+    mine = p.shape[1]
+    skip = out.shape[0] - mine
+    share = jnp.where(odd == 1, out[skip:, :], out[:mine, :])
+    for b in range(n):
+        e = (b + 1) * B
+        p[b * B:e, :] = dot(w[b * B:e, :e], share[:, :e], NT)
     for stream in streams.values():
         stream.finish()
 
 
-def finish(slab, s):
+def whole(t, slab):
+    d, K = t.shape
+    R = slab.shape[0]
+    plan, count, _ = sketch_plan(d, K // 128 * 2 // 5 * 128, K)
+    C, rows = NZ * NY * d, NY * d
     bf = jnp.bfloat16
-    C, R = s.shape
     vm = lambda *shape: pltpu.VMEM(shape, F32)
+    HBM = pl.BlockSpec(memory_space=pltpu.HBM)
     return pl.pallas_call(
-        finish_kernel,
-        out_shape=(jax.ShapeDtypeStruct((144, C), F32), jax.ShapeDtypeStruct((C, C), F32)),
-        in_specs=[VM, VM], out_specs=(VM, VM),
+        functools.partial(whole_kernel, plan),
+        out_shape=jax.ShapeDtypeStruct((C, K // (NZ * NY)), F32),
+        in_specs=[HBM, HBM], out_specs=VM,
         scratch_shapes=[
+            pltpu.VMEM((R, K), bf), DMA, vm(C, R), pltpu.VMEM((C // 8, 8, K), bf),
+            vm(NZ, rows, R), vm(NZ, rows, R // 2), vm(NZ, rows, R // 2), vm(NZ, NX, rows, R // 2),
+            DMA((count,)), DMA((count,)), DMA((40,)), DMA((40,)), DMA,
+            vm(144, C), vm(C, C),
             vm(NZ, 560, C), vm(560, HALF), vm(NZ, 144, HALF),
             *[vm(NZ - 1, n, HALF) for _, _, n in Z_ROWS],
             *[vm(NY - 1, NZ, n, HALF) for _, _, n in Y_ROWS],
@@ -611,15 +612,12 @@
             *GRAM_SCRATCH, vm(NX, 2, SLOTS * B, B), vm(C, C), vm(C, C), vm(B, 2 * B), vm(B, B),
             DMA((RS_COPIES,)), DMA((RS_COPIES,)), DMA((GRAM_COPIES,)), DMA((GRAM_COPIES,)),
         ],
-        compiler_params=pltpu.CompilerParams(collective_id=2, has_side_effects=True, vmem_limit_bytes=60 * 2**20), name="finish",
-    )(slab, s)
+        compiler_params=pltpu.CompilerParams(collective_id=0, has_side_effects=True, vmem_limit_bytes=63 * 2**20), name="whole",
+    )(t.reshape(d // 8, 8, K), slab)
 
 
 def body(slab, test):
-    c, w = finish(slab, sketch_of(test.T, slab))
-    y = lax.axis_index("y")
-    c = lax.dynamic_slice_in_dim(c, y * 140 % 8, 140, 0)
-    p = lax.dot_general(w, c, (NT, ((), ())), precision=HI, preferred_element_type=F32)
+    p = whole(test.T, slab)
     p = lax.all_to_all(p.reshape(NZ * NY, 24, -1), ("z", "y"), 0, 0, tiled=True)
     return p.transpose(1, 0, 2).reshape(24, -1)
 

time: 207 us -> 195 us (0.942)
  Pallas kernels: 174 us -> 168 us
  matrix products: 3.74 us -> 0 us
  local copies, waits for them, and re-layouts: 4.86 us -> 1.39 us
    pallas_call x2 -> x1, Pallas kernels: 174 us -> 168 us  [whole(): pl.pallas_call(functools.partial(whole_kernel, plan), out_shape=jax.Shape...]
    dot_general x1 -> x0, matrix products: 3.74 us -> none  [body(): lax.dot_general(w, c, (NT, ((), ())), precision=HI, preferred_element_typ...]
    unnamed x6 -> x0, local copies, waits for them, and re-layouts: 3.46 us -> none
where the time goes in v4:
time: 195 us; the launch traced here: 194 us
  Pallas kernels  168 us (86%)
  blocking collectives  24.5 us (13%)
    pallas_call x1, Pallas kernels, whole(): pl.pallas_call(functools.partial(whole_kernel, plan), out_shape=jax.Shape...  168 us
    all_to_all x1, blocking collectives, body(): p = lax.all_to_all(p.reshape(NZ * NY, 24, -1), ('z', 'y'), 0, 0, tiled=True)  24.5 us

profile of v4, /device:TPU:8, one launch (start us, length us, event | category | flops | bytes accessed | tf_op | source)
XLA Modules:
  0.0 194.4 jit_solution(11784628340008199222)
XLA Ops:
  0.0 168.5 %whole.1 = f32[768,140]{1,0:T(8,128)} custom-call(bf16[3,8,4480]{2,1,0:T(8,128)(2,1)} %bitcast.7, bf16[256,4480]{1,0:T(8,128)(2,1)} %slab_in.1), custom_call_target="tpu_custom_call" | custom-call | tf_op jit(solution)/shard_map/whole/pallas_call | solution.py:597
  168.5 24.5 %all_to_all.5 = f32[32,24,140]{2,1,0:T(8,128)S(1)} all-to-all(f32[32,24,140]{2,1,0:T(8,128)} %bitcast.6), channel_id=1, replica_groups=mesh['z'=8,'y'=4,'x'=4,'c'=2] {'z','y'}, dimensions={0} | all-to-all | bytes 860160 | tf_op jit(solution)/shard_map/all_to_all | solution.py:621
  193.0 0.3 copy.3
  193.2 1.1 reshape.11

commit v5 on v4

--- a/solution.py
+++ b/solution.py
@@ -335,6 +335,8 @@
 Y_ROWS = ((1, 0, 40), (1, 40, 32), (-1, 72, 40), (-1, 112, 32))
 ZY_ROWS = ((1, 0, 72), (-1, 72, 72))
 HALF = 384
+WIDTH = 140
+REST = WIDTH - 128
 KINDS = (("z", "z", Z_ROWS), ("y", "y", Y_ROWS), ("zy", "y", ZY_ROWS), ("yz", "z", Y_ROWS))
 
 
@@ -494,8 +496,6 @@
         return 0
 
     start = lax.rem(lax.axis_index("z") + NZ - 1, NZ) * (slab.shape[1] // NZ) // B
-    early = 15
-
     def tiles_of(lo, hi):
         lax.fori_loop(lo, hi, lambda t, _: tile(lax.rem(start + t, tiles), 0), 0)
 
@@ -533,7 +533,7 @@
         elif what[0] == "serve":
             streams[what[1]].serve(what[2])
         elif what[0] == "tiles":
-            tiles_of(early, tiles)
+            tiles_of(14, tiles)
 
     plan = finish_plan()[0]
     first = next(i for i, what in enumerate(plan) if what[0] == "chol")
@@ -547,9 +547,14 @@
         else:
             table.setdefault(key, []).append(what)
 
-    tiles_of(0, early)
+    tiles_of(0, 3)
+    streams["z", 0].copy(0).start()
+    tiles_of(10, 14)
+    streams["z", 2].copy(0).start()
+    tiles_of(3, 10)
     w[...] = jnp.zeros_like(w)
-    for what in plan[:first]:
+    p[:, 24:, :] = jnp.zeros((p.shape[0], 8, 128), F32)
+    for what in plan[1:first]:
         act(what)
     row_of = lax.broadcasted_iota(jnp.int32, (B, B), 0)
     col_of = lax.broadcasted_iota(jnp.int32, (B, B), 1)
@@ -573,15 +578,37 @@
         return 0
 
     lax.fori_loop(0, n, step, 0)
-    for what in plan[last + 1:]:
+    odd = lax.rem(lax.axis_index("y"), 2)
+    skip = out.shape[0] - WIDTH
+
+    def share(lo, hi):
+        return jnp.where(odd == 1, out[skip:, lo:hi], out[:WIDTH, lo:hi])
+
+    def put(b, value):
+        for q in range(B // 8):
+            to, i = divmod(b * (B // 8) + q, 3)
+            p[to, 8 * i:8 * i + 8, :] = value[8 * q:8 * q + 8, :128]
+            p[to, 24:, REST * i:REST * i + REST] = value[8 * q:8 * q + 8, 128:]
+
+    rest_of_plan = plan[last + 1:]
+    ready = 1 + max([i for i, what in enumerate(rest_of_plan) if what[0] == "serve" and what[1][0] == "zy"], default=-1)
+    for what in rest_of_plan[:ready]:
         act(what)
-    odd = lax.rem(lax.axis_index("y"), 2)
-    mine = p.shape[1]
-    skip = out.shape[0] - mine
-    share = jnp.where(odd == 1, out[skip:, :], out[:mine, :])
+    half = share(0, HALF)
+    begun = {}
     for b in range(n):
-        e = (b + 1) * B
-        p[b * B:e, :] = dot(w[b * B:e, :e], share[:, :e], NT)
+        e = min((b + 1) * B, HALF)
+        begun[b] = dot(w[b * B:(b + 1) * B, :e], half[:, :e], NT)
+        if b < HALF // B:
+            put(b, begun[b])
+        else:
+            a[b * B:(b + 1) * B, :WIDTH] = begun[b]
+    for what in rest_of_plan[ready:]:
+        act(what)
+    half = share(HALF, 2 * HALF)
+    for b in range(HALF // B, n):
+        e = (b + 1) * B - HALF
+        put(b, a[b * B:(b + 1) * B, :WIDTH] + dot(w[b * B:(b + 1) * B, HALF:HALF + e], half[:, :e], NT))
     for stream in streams.values():
         stream.finish()
 
@@ -596,7 +623,7 @@
     HBM = pl.BlockSpec(memory_space=pltpu.HBM)
     return pl.pallas_call(
         functools.partial(whole_kernel, plan),
-        out_shape=jax.ShapeDtypeStruct((C, K // (NZ * NY)), F32),
+        out_shape=jax.ShapeDtypeStruct((NZ * NY, d + 8, 128), F32),
         in_specs=[HBM, HBM], out_specs=VM,
         scratch_shapes=[
             pltpu.VMEM((R, K), bf), DMA, vm(C, R), pltpu.VMEM((C // 8, 8, K), bf),
@@ -616,10 +643,20 @@
     )(t.reshape(d // 8, 8, K), slab)
 
 
+def unpack_kernel(q, out):
+    for k in range(q.shape[0]):
+        out[:, WIDTH * k:WIDTH * k + 128] = q[k, :24, :]
+        for i in range(3):
+            out[8 * i:8 * i + 8, WIDTH * k + 128:WIDTH * (k + 1)] = q[k, 24:, REST * i:REST * i + REST]
+
+
 def body(slab, test):
     p = whole(test.T, slab)
-    p = lax.all_to_all(p.reshape(NZ * NY, 24, -1), ("z", "y"), 0, 0, tiled=True)
-    return p.transpose(1, 0, 2).reshape(24, -1)
+    q = lax.all_to_all(p, ("z", "y"), 0, 0, tiled=True)
+    return pl.pallas_call(
+        unpack_kernel, out_shape=jax.ShapeDtypeStruct((24, slab.shape[1]), F32),
+        in_specs=[VM], out_specs=VM, name="unpack",
+    )(q)
 
 
 def solution(mesh):

time: 195 us -> 190 us (0.974)
  blocking collectives: 24.5 us -> 20.1 us
  Pallas kernels: 168 us -> 170 us
    all_to_all x1, blocking collectives: 24.5 us -> 20.1 us  [body(): q = lax.all_to_all(p, ('z', 'y'), 0, 0, tiled=True)]
    pallas_call x0 -> x1, Pallas kernels: none -> 2.06 us  [body(): pl.pallas_call(unpack_kernel, out_shape=jax.ShapeDtypeStruct((24, slab.sh...]
where the time goes in v5:
time: 190 us
  Pallas kernels  170 us (89%)
  blocking collectives  20.1 us (11%)
    pallas_call x1, Pallas kernels, whole(): pl.pallas_call(functools.partial(whole_kernel, plan), out_shape=jax.Shape...  168 us
    all_to_all x1, blocking collectives, body(): q = lax.all_to_all(p, ('z', 'y'), 0, 0, tiled=True)  20.1 us

profile of v5, /device:TPU:8, one launch (start us, length us, event | category | flops | bytes accessed | tf_op | source)
XLA Modules:
  0.0 189.9 jit_solution(11856917699846682290)
XLA Ops:
  0.0 167.7 %whole.1 = f32[32,32,128]{2,1,0:T(8,128)} custom-call(bf16[3,8,4480]{2,1,0:T(8,128)(2,1)} %bitcast.3, bf16[256,4480]{1,0:T(8,128)(2,1)} %slab_in.1), custom_call_target="tpu_custom_call" | custom-call | tf_op jit(solution)/shard_map/whole/pallas_call | solution.py:624
  167.7 20.1 %all_to_all.5.q = f32[32,32,128]{2,1,0:T(8,128)} all-to-all(f32[32,32,128]{2,1,0:T(8,128)} %whole.1), channel_id=1, replica_groups=mesh['z'=8,'y'=4,'x'=4,'c'=2] {'z','y'}, dimensions={0} | all-to-all | bytes 1048576 | tf_op jit(solution)/shard_map/all_to_all | solution.py:655
  187.8 2.1 %unpack.1 = f32[24,4480]{1,0:T(8,128)} custom-call(f32[32,32,128]{2,1,0:T(8,128)} %all_to_all.5.q), custom_call_target="tpu_custom_call" | custom-call | tf_op jit(solution)/shard_map/unpack/pallas_call | solution.py:656
